TPU v7x, 1024 devices: a whole 4x4x32 slice. The times are simulated.
1024 devices in a mesh: seq: 8 (over x, core), chan: 128 (over y, z).
Axes of the slice: x: 4, y: 4, z: 32, core: 2. Of those that a mesh axis runs over, the one named last changes fastest.
Arguments:
- projections: bfloat16 [3, 2048, 16384], P(None, 'chan', 'seq'), may hold values from -6 to 6
- filter_taps: float32 [2048, 16384], P('chan', 'seq'), may hold values from -1.3 to 1.3
- skip_gain: float32 [2048], P('chan'), may hold values from -1 to 1
- head_weight: bfloat16 [2048, 3840], P('chan'), may hold values from -0.75 to 0.75
- head_bias: float32 [3840], replicated, may hold values from -1 to 1
- counts: int32 [512, 3840], P('seq'), may hold values from 0 to 11
Outputs:
- mean_loss: float32 [], replicated
- feature_grads: float32 [3, 2048, 16384], P(None, 'chan', 'seq')
All inputs are finite; a program needn't handle non-finite values.
Results may differ from a plain program's by a relative error of at most 0.007.
Values may be sent and summed in bfloat16 or wider, within the bound.
A program may use at most 32 MiB of HBM per device.

v0:
```python
import math

import jax
import jax.numpy as jnp
from jax import lax
from jax.sharding import PartitionSpec as P

POOL = 32


total_weight = 0.2
rate_floor = 0.5


def split_length(padded_len):
    best = 1
    factor = 1
    while factor * factor <= padded_len:
        if padded_len % factor == 0:
            best = factor
        factor = factor + 1
    return (padded_len // best, best)


def dft_tables(outer, inner, padded_len):
    outer_idx = jnp.arange(outer, dtype=jnp.int32)
    inner_idx = jnp.arange(inner, dtype=jnp.int32)
    outer_angle = (
        2.0
        * math.pi
        * (outer_idx[:, None] * outer_idx[None, :] % outer).astype(jnp.float32)
        / outer
    )
    inner_angle = (
        2.0
        * math.pi
        * (inner_idx[:, None] * inner_idx[None, :] % inner).astype(jnp.float32)
        / inner
    )
    twist_angle = (
        2.0
        * math.pi
        * (outer_idx[:, None] * inner_idx[None, :] % padded_len).astype(jnp.float32)
        / padded_len
    )
    return (
        jnp.cos(outer_angle),
        -jnp.sin(outer_angle),
        jnp.cos(inner_angle),
        -jnp.sin(inner_angle),
        jnp.cos(twist_angle),
        -jnp.sin(twist_angle),
    )


def forward(real_in, tables):
    outer_re, outer_im, inner_re, inner_im, twist_re, twist_im = tables
    highest = lax.Precision.HIGHEST
    first_re = jnp.einsum("ka,mab->mkb", outer_re, real_in, precision=highest)
    first_im = jnp.einsum("ka,mab->mkb", outer_im, real_in, precision=highest)
    turned_re = first_re * twist_re - first_im * twist_im
    turned_im = first_re * twist_im + first_im * twist_re
    spec_re = jnp.einsum("mkb,bj->mkj", turned_re, inner_re, precision=highest) - jnp.einsum(
        "mkb,bj->mkj", turned_im, inner_im, precision=highest
    )
    spec_im = jnp.einsum("mkb,bj->mkj", turned_re, inner_im, precision=highest) + jnp.einsum(
        "mkb,bj->mkj", turned_im, inner_re, precision=highest
    )
    return (spec_re, spec_im)


def inverse(spec_re, spec_im, tables, padded_len):
    outer_re, outer_im, inner_re, inner_im, twist_re, twist_im = tables
    highest = lax.Precision.HIGHEST
    back_re = jnp.einsum("mkj,bj->mkb", spec_re, inner_re, precision=highest) + jnp.einsum(
        "mkj,bj->mkb", spec_im, inner_im, precision=highest
    )
    back_im = jnp.einsum("mkj,bj->mkb", spec_im, inner_re, precision=highest) - jnp.einsum(
        "mkj,bj->mkb", spec_re, inner_im, precision=highest
    )
    turned_re = back_re * twist_re + back_im * twist_im
    turned_im = back_im * twist_re - back_re * twist_im
    result = jnp.einsum("ka,mkb->mab", outer_re, turned_re, precision=highest) + jnp.einsum(
        "ka,mkb->mab", outer_im, turned_im, precision=highest
    )
    return result / padded_len


def to_pencil(stacked):
    return lax.all_to_all(stacked, "seq", split_axis=1, concat_axis=2, tiled=True)


def from_pencil(pencil_rows):
    return lax.all_to_all(pencil_rows, "seq", split_axis=1, concat_axis=0, tiled=True)


def pad_fold(pencil, outer, inner):
    padded = jnp.concatenate([pencil, jnp.zeros_like(pencil)], axis=2)
    return padded.reshape(-1, outer, inner)


def per_device(projections, filter_taps, skip_gain, head_weight, head_bias, counts):
    query = projections[0].astype(jnp.float32)
    keyed = projections[1].astype(jnp.float32)
    valued = projections[2].astype(jnp.float32)
    channels, width = keyed.shape
    bins = width // POOL
    seq_count = lax.axis_size("seq")
    tracks = head_weight.shape[1]
    key_value = keyed * valued
    pencil = to_pencil(jnp.stack([key_value, filter_taps], axis=0))
    pencil_ch = pencil.shape[1]
    length = pencil.shape[2]
    padded_len = 2 * length
    outer, inner = split_length(padded_len)
    tables = dft_tables(outer, inner, padded_len)
    spec_re, spec_im = forward(pad_fold(pencil, outer, inner), tables)
    signal_re = spec_re[:pencil_ch]
    signal_im = spec_im[:pencil_ch]
    taps_re = spec_re[pencil_ch:]
    taps_im = spec_im[pencil_ch:]
    prod_re = signal_re * taps_re - signal_im * taps_im
    prod_im = signal_re * taps_im + signal_im * taps_re
    conv_pencil = inverse(prod_re, prod_im, tables, padded_len).reshape(pencil_ch, padded_len)[
        :, :length
    ]
    conv = from_pencil(conv_pencil)
    mixed = conv + skip_gain[:, None] * key_value
    output = query * mixed
    pooled = output.reshape(channels, bins, POOL).mean(axis=2).astype(jnp.bfloat16)
    partial_value = jnp.einsum("cb,ct->bt", pooled, head_weight, preferred_element_type=jnp.float32)
    logits = lax.psum(partial_value, "chan") + head_bias[None, :]
    rates = jax.nn.softplus(logits) + rate_floor
    observed = counts.astype(jnp.float32)
    local_log = jnp.sum(observed * jnp.log(rates))
    pred_total, obs_total, log_sum = lax.psum(
        (jnp.sum(rates, axis=0), jnp.sum(observed, axis=0), local_log), "seq"
    )
    log_pred = jnp.log(pred_total)
    loss_sum = (
        jnp.sum(total_weight * (pred_total - obs_total * log_pred) + obs_total * log_pred) - log_sum
    )
    ratio = obs_total / pred_total
    grad_rates = total_weight * (1.0 - ratio)[None, :] + ratio[None, :] - observed / rates
    grad_logits = (grad_rates * jax.nn.sigmoid(logits)).astype(jnp.bfloat16)
    grad_pooled = jnp.einsum(
        "bt,ct->cb", grad_logits, head_weight, preferred_element_type=jnp.float32
    )
    mean_loss = loss_sum / (bins * seq_count * tracks)
    grad_output = jnp.broadcast_to(grad_pooled[:, :, None] / POOL, (channels, bins, POOL)).reshape(
        channels, width
    )
    grad_query = grad_output * mixed
    gated = grad_output * query
    back_pencil = to_pencil(gated[None])
    back_re, back_im = forward(pad_fold(back_pencil, outer, inner), tables)
    corr_re = taps_re * back_re + taps_im * back_im
    corr_im = taps_re * back_im - taps_im * back_re
    corr_pencil = inverse(corr_re, corr_im, tables, padded_len).reshape(pencil_ch, padded_len)[
        :, :length
    ]
    grad_kv = from_pencil(corr_pencil) + skip_gain[:, None] * gated
    return (mean_loss, jnp.stack([grad_query, grad_kv * valued, grad_kv * keyed], axis=0))


def solution(mesh):
    placed = (
        P(None, "chan", "seq"),
        P("chan", "seq"),
        P("chan"),
        P("chan", None),
        P(),
        P("seq", None),
    )
    return jax.shard_map(
        per_device,
        mesh=mesh,
        in_specs=placed,
        out_specs=(P(), P(None, "chan", "seq")),
        check_vma=False,
    )
```

profile of v0, /device:TPU:1, one launch (start us, length us, event | category | flops | bytes accessed | tf_op | source)
XLA Modules:
  0.0 639.6 jit_solution(16308448738495438297)
XLA Ops:
  7.2 1.0 convert_multiply_fusion.1
  8.2 0.9 copy.40
  9.1 17.4 %all-to-all-start = ((f32[2,16,2048]{2,0,1:T(2,128)}), f32[2,16,2048]{2,0,1:T(2,128)S(1)}, u32[]{:S(2)}, u32[]{:S(2)}) async-start(f32[2,16,2048]{2,0,1:T(2,128)} %copy.40), calls=%async_computation | async-start | bytes 524288 | tf_op jit(solution)/shard_map/all_to_all | solution.py:90
  27.3 5.8 all-to-all-done
  34.0 1.8 convolution_bitcast_fusion
  35.9 1.8 convolution_bitcast_fusion.1
  37.7 1.2 fusion.88
  38.9 1.2 fusion.73
  40.1 1.2 convolution_subtract_fusion
  41.4 1.2 convolution_add_fusion
  43.9 0.8 convolution_add_fusion.5
  45.4 1.5 fusion.20
  46.8 1.5 fusion.3
  48.7 0.7 slice.40
  49.4 4.4 all-to-all-start.1
  54.2 4.9 all-to-all-done.1
  60.0 1.3 fusion.104
  61.5 486.5 %all-reduce.5.cloned.1.call-done = f32[64,3840]{1,0:T(8,128)} async-done(((f32[64,3840]{1,0:T(8,128)}), f32[64,3840]{1,0:T(8,128)}) %all-reduce.5.cloned.1.call-update) | async-done | bytes 983056 | tf_op jit(solution)/shard_map/psum | solution.py:132
  548.0 2.7 multiply_reduce_fusion
  550.7 44.2 %all-reduce.2 = (f32[3840]{0:T(1024)S(1)}, f32[3840]{0:T(1024)S(1)}, f32[]{:T(128)}) all-reduce(f32[3840]{0:T(1024)S(1)} %get-tuple-element.3, f32[3840]{0:T(1024)S(1)} %get-tuple-element.4, f32[]{:T(128)} %get-tuple-element.2), channel_id=1, replica_groups=mesh['seq'=8,'chan'=128] {'seq'}, use_global_device_ids=true, to_apply=%region_3.4 | all-reduce | flops 7681 | bytes 61448 | tf_op jit(solution)/shard_map/psum | solution.py:136
  594.9 0.7 multiply_add_fusion.7
  595.6 2.2 fusion.4
  598.5 10.8 %all_to_all.77 = f32[1,16,2048]{2,0,1:T(1,128)S(1)} all-to-all(f32[1,16,2048]{2,0,1:T(1,128)S(1)} %copy.54), channel_id=1, replica_groups=mesh['seq'=8,'chan'=128] {'seq'}, dimensions={1} | all-to-all | bytes 262144 | tf_op jit(solution)/shard_map/all_to_all | solution.py:90
  609.5 1.4 convolution_bitcast_fusion.2
  610.9 1.4 convolution_bitcast_fusion.3
  614.1 0.7 multiply_add_fusion.1
  617.3 1.5 fusion.17
  618.8 1.5 fusion.1
  620.6 0.7 slice.41
  621.3 4.2 all-to-all-start.3
  626.8 3.9 all-to-all-done.3
  630.9 0.8 pad_maximum_fusion
  (52 shorter events, 11.2 us)
Async XLA Ops:
  7.2 52.9 %copy-start = (bf16[16,3840]{1,0:T(8,128)(2,1)S(1)}, bf16[16,3840]{1,0:T(8,128)(2,1)}, u32[]{:S(2)}) copy-start(bf16[16,3840]{1,0:T(8,128)(2,1)} %param.9) | copy-start | bytes 368644
  7.2 1.0 copy-start.3
  9.1 23.9 %all-to-all-start = ((f32[2,16,2048]{2,0,1:T(2,128)}), f32[2,16,2048]{2,0,1:T(2,128)S(1)}, u32[]{:S(2)}, u32[]{:S(2)}) async-start(f32[2,16,2048]{2,0,1:T(2,128)} %copy.40), calls=%async_computation | async-start | bytes 524288 | tf_op jit(solution)/shard_map/all_to_all | solution.py:90
  49.4 4.5 copy-start.1
  49.4 9.7 %all-to-all-start.1 = ((f32[2,8,2048]{2,0,1:T(2,128)}), f32[2,8,2048]{2,0,1:T(2,128)S(1)}, u32[]{:S(2)}, u32[]{:S(2)}) async-start(f32[2,8,2048]{2,0,1:T(2,128)} %bitcast.10), calls=%async_computation.1 | async-start | bytes 262144 | tf_op jit(solution)/shard_map/all_to_all | solution.py:94
  53.8 494.2 %all-reduce.5.cloned.1.call-start = ((), (), s32[]{:S(2)}) async-start(), calls=%async_computation.4 | async-start | bytes 1966080 | tf_op jit(solution)/shard_map/psum | solution.py:132
  59.1 0.7 copy-start.5
  60.0 488.0 %copy-start.2 = (s32[64,3840]{1,0:T(8,128)S(1)}, s32[64,3840]{1,0:T(8,128)}, u32[]{:S(2)}) copy-start(s32[64,3840]{1,0:T(8,128)} %param.11) | copy-start | bytes 2949124
  61.4 486.6 %copy-start.4 = (f32[3840]{0:T(1024)S(1)}, f32[3840]{0:T(1024)}, u32[]{:S(2)}) copy-start(f32[3840]{0:T(1024)} %param.10) | copy-start | bytes 46084
  621.3 9.4 %all-to-all-start.3 = ((f32[2,8,2048]{2,0,1:T(2,128)}), f32[2,8,2048]{2,0,1:T(2,128)S(1)}, u32[]{:S(2)}, u32[]{:S(2)}) async-start(f32[2,8,2048]{2,0,1:T(2,128)} %bitcast.18), calls=%async_computation.3 | async-start | bytes 262144 | tf_op jit(solution)/shard_map/all_to_all | solution.py:94
Sparse Core Ops, SparseCore 0:
  61.5 486.4 all-reduce.4
where the time goes:
time: 640 us
  waiting for transfers between devices  501 us (78%)
  blocking collectives  55 us (9%)
  matrix products  28.3 us (4%)
  starting transfers between devices  26 us (4%)
  between operations  16.9 us (3%)
    psum x1, waiting for transfers between devices, per_device(): logits = lax.psum(partial_value, 'chan') + head_bias[None, :]  486 us
    psum x1, blocking collectives, per_device(): lax.psum((jnp.sum(rates, axis=0), jnp.sum(observed, axis=0), local_log),...  44.2 us
    all_to_all x1, starting transfers between devices, to_pencil(): lax.all_to_all(stacked, 'seq', split_axis=1, concat_axis=2, tiled=True)  17.4 us
  transfers between devices with their start and end apart: 4, of which 4 were waited for; matrix products, arithmetic and copies ran while one was open for 0% of the time, Pallas kernels for 0%

commit v1 on v0

--- a/solution.py
+++ b/solution.py
@@ -3,13 +3,241 @@
 import jax
 import jax.numpy as jnp
 from jax import lax
+from jax.experimental import pallas as pl
+from jax.experimental.pallas import tpu as pltpu
 from jax.sharding import PartitionSpec as P
 
 POOL = 32
-
+NY = 4
+NZ = 32
+NS = 8
+TR = 120
+MESH = pl.DeviceIdType.MESH
 
 total_weight = 0.2
 rate_floor = 0.5
+
+
+def head_kernel(
+    w_ref, p_ref, cnt_ref, bias_ref,
+    gp_ref, loss_ref,
+    wa, wg, py, pg, ty, ts, gg,
+    s_loc, s_wa, r_wa, s_wb, r_wb, s_wy, r_wy, s_py, r_py, s_pf, r_pf, s_pn, r_pn,
+    s_ty, r_ty, s_ts, r_ts, s_gf, r_gf, s_gn, r_gn, s_gy, r_gy,
+):
+    s = lax.axis_index("seq")
+    ch = lax.axis_index("chan")
+    y = ch // NZ
+    z = ch % NZ
+
+    def zdev(d):
+        return (s, y * NZ + (z + d + NZ) % NZ)
+
+    def ydev(d):
+        return (s, ((y + d) % NY) * NZ + z)
+
+    def sdev(d):
+        return ((s + d) % NS, ch)
+
+    def send(src, dst, ss, rs, dev):
+        c = pltpu.make_async_remote_copy(
+            src_ref=src, dst_ref=dst, send_sem=ss, recv_sem=rs, device_id=dev, device_id_type=MESH
+        )
+        c.start()
+        return c
+
+    near = ((0, -1), (2, 1), (3, 2))
+
+    barrier = pltpu.get_barrier_semaphore()
+    peers = [sdev(d) for d in range(1, NS)] + [ydev(d) for d in range(1, NY)]
+    peers += [zdev(4 * k) for k in range(1, 8)] + [zdev(d) for d in (-2, -1, 1, 2)]
+    for dev in peers:
+        pl.semaphore_signal(barrier, inc=1, device_id=dev, device_id_type=MESH)
+    pl.semaphore_wait(barrier, len(peers))
+
+    c_wa = [send(w_ref.at[:, m], wa.at[m], s_wa.at[m], r_wa.at[m], zdev(o)) for m, o in near]
+    c_py = [
+        send(p_ref.at[d], py.at[d - 1], s_py.at[d], r_py.at[d], ydev(d)) for d in range(1, NY)
+    ]
+    own = pltpu.make_async_copy(w_ref.at[:, 1], wa.at[1], s_loc.at[0])
+    own.start()
+    own.wait()
+    for c in c_wa:
+        c.wait_recv()
+    c_wb = [
+        send(wa.at[:, k], wg.at[0, k], s_wb.at[k], r_wb.at[k], zdev(4 * k)) for k in range(1, 8)
+    ]
+    own = pltpu.make_async_copy(wa.at[:, 0], wg.at[0, 0], s_loc.at[1])
+    own.start()
+
+    for c in c_py:
+        c.wait_recv()
+    tile = p_ref[0].astype(jnp.float32)
+    for d in range(NY - 1):
+        tile = tile + py[d].astype(jnp.float32)
+    pg[1, 0] = tile.astype(jnp.bfloat16)
+    c_pf = [
+        send(pg.at[1, 0], pg.at[1, k], s_pf.at[k], r_pf.at[k], zdev(4 * k)) for k in range(1, 8)
+    ]
+    for c in c_pf:
+        c.wait_recv()
+    c_pn = [send(pg.at[1], pg.at[m], s_pn.at[m], r_pn.at[m], zdev(o)) for m, o in near]
+
+    own.wait()
+    for c in c_wb:
+        c.wait_recv()
+    c_wy = [
+        send(wg.at[0], wg.at[d], s_wy.at[d], r_wy.at[d], ydev(d)) for d in range(1, NY)
+    ]
+    for c in c_pn:
+        c.wait_recv()
+    for c in c_wy:
+        c.wait_recv()
+
+    logits = jnp.broadcast_to(bias_ref[0:1, :], (16, 128))
+    for k in range(8):
+        for m in range(4):
+            rows = jnp.concatenate([wg[d, k, m] for d in range(NY)], axis=0)
+            logits = logits + lax.dot_general(
+                pg[m, k][:, :64], rows, (((1,), (0,)), ((), ())),
+                preferred_element_type=jnp.float32,
+            )
+    rates = jnp.maximum(logits, 0.0) + jnp.log1p(jnp.exp(-jnp.abs(logits))) + rate_floor
+    observed = cnt_ref[...].astype(jnp.float32)
+    part = [
+        jnp.sum(rates, axis=0, keepdims=True),
+        jnp.sum(observed, axis=0, keepdims=True),
+        jnp.sum(observed * jnp.log(rates), axis=0, keepdims=True),
+        jnp.zeros((5, 128), jnp.float32),
+    ]
+    ty[0] = jnp.concatenate(part, axis=0)
+    c_ty = [send(ty.at[0], ty.at[d], s_ty.at[d], r_ty.at[d], ydev(d)) for d in range(1, NY)]
+    sig = 1.0 / (1.0 + jnp.exp(-logits))
+    obs_rate = observed / rates
+    for c in c_ty:
+        c.wait_recv()
+    tot = ty[y]
+    for a in range(1, NY):
+        tot = tot + ty[(y + NY - a) % NY]
+    ts[0] = tot
+    c_ts = [send(ts.at[0], ts.at[d], s_ts.at[d], r_ts.at[d], sdev(d)) for d in range(1, NS)]
+    for c in c_ts:
+        c.wait_recv()
+    tot = ts[s]
+    for a in range(1, NS):
+        tot = tot + ts[(s + NS - a) % NS]
+    pred = tot[0:1, :]
+    obs = tot[1:2, :]
+    log_pred = jnp.log(pred)
+    lane = lax.broadcasted_iota(jnp.int32, (1, 128), 1)
+    terms = total_weight * (pred - obs * log_pred) + obs * log_pred - tot[2:3, :]
+    loss = jnp.sum(jnp.where(lane < TR, terms, 0.0), axis=1, keepdims=True)
+    ratio = obs / pred
+    grad_rates = total_weight * (1.0 - ratio) + ratio - obs_rate
+    grad = grad_rates * sig
+    hi = loss.astype(jnp.bfloat16).astype(jnp.float32)
+    mid = (loss - hi).astype(jnp.bfloat16).astype(jnp.float32)
+    lo = loss - hi - mid
+    lanes = lax.broadcasted_iota(jnp.int32, (16, 128), 1)
+    grad = jnp.where(
+        lanes < TR, grad, jnp.where(lanes == TR, hi, jnp.where(lanes == TR + 1, mid, lo))
+    )
+    gg[0, 1, 0] = grad.astype(jnp.bfloat16)
+    c_gf = [
+        send(gg.at[0, 1, 0], gg.at[0, 1, k], s_gf.at[k], r_gf.at[k], zdev(-4 * k))
+        for k in range(1, 8)
+    ]
+    for c in c_gf:
+        c.wait_recv()
+    c_gn = [
+        send(gg.at[0, 1], gg.at[0, m], s_gn.at[m], r_gn.at[m], zdev(-o)) for m, o in near
+    ]
+    c_gy = [
+        send(gg.at[0, 1], gg.at[d, 1], s_gy.at[d, 1], r_gy.at[d, 1], ydev(d))
+        for d in range(1, NY)
+    ]
+    for c, (m, o) in zip(c_gn, near):
+        c.wait_recv()
+        c_gy += [
+            send(gg.at[0, m], gg.at[d, m], s_gy.at[d, m], r_gy.at[d, m], ydev(d))
+            for d in range(1, NY)
+        ]
+
+    by_z = jnp.zeros((1, 128), jnp.float32)
+    for k in range(8):
+        for m in range(4):
+            row = gg[0, m, k][0:1, :].astype(jnp.float32)
+            val = jnp.sum(
+                jnp.where((lane >= TR) & (lane < TR + 3), row, 0.0), axis=1, keepdims=True
+            )
+            by_z = jnp.where(lane == (z + m - 1 + 4 * k + NZ) % NZ, val, by_z)
+    loss_ref[...] = jnp.broadcast_to(jnp.sum(by_z, axis=1, keepdims=True), (8, 128))
+
+    wl = jnp.concatenate([w_ref[k, m] for k in range(8) for m in range(4)], axis=1)
+
+    def grad_block(d):
+        gl = jnp.concatenate([gg[d, m, k] for k in range(8) for m in range(4)], axis=1)
+        return lax.dot_general(
+            wl, gl, (((1,), (1,)), ((), ())), preferred_element_type=jnp.float32
+        )
+
+    gp_ref[0] = grad_block(0)
+    for c in c_gy:
+        c.wait_recv()
+    for d in range(1, NY):
+        gp_ref[d] = grad_block(d)
+
+    for c in c_wa + c_py + c_wb + c_pf + c_pn + c_wy + c_ty + c_ts + c_gf + c_gn + c_gy:
+        c.wait_send()
+
+
+def head(pooled, head_weight, head_bias, counts):
+    ch = lax.axis_index("chan")
+    y = ch // NZ
+    z = ch % NZ
+    w = jnp.pad(head_weight.reshape(16, NZ, TR), ((0, 0), (0, 0), (0, 128 - TR)))
+    w = jnp.transpose(w, (1, 0, 2))
+    w = lax.dynamic_slice_in_dim(jnp.concatenate([w, w], axis=0), (z + NZ - 1) % NZ, NZ, 0)
+    w = w.reshape(8, 4, 16, 128)
+    pt = pooled.T
+    pt = lax.dynamic_slice_in_dim(jnp.concatenate([pt, pt], axis=0), y * 16, 64, 0)
+    pt = pt.reshape(NY, 16, 16)
+    pt = jnp.stack([jnp.pad(pt[d], ((0, 0), (16 * d, 112 - 16 * d))) for d in range(NY)])
+    cnt = lax.dynamic_slice(counts, (y * 16, z * TR), (16, TR))
+    cnt = jnp.pad(cnt, ((0, 0), (0, 128 - TR)))
+    bias = jnp.pad(lax.dynamic_slice_in_dim(head_bias, z * TR, TR, 0), (0, 128 - TR))
+    bias = jnp.broadcast_to(bias[None, :], (8, 128))
+    sem = pltpu.SemaphoreType.DMA
+    b16 = jnp.bfloat16
+    gp, loss = pl.pallas_call(
+        head_kernel,
+        out_shape=(
+            jax.ShapeDtypeStruct((NY, 16, 16), jnp.float32),
+            jax.ShapeDtypeStruct((8, 128), jnp.float32),
+        ),
+        in_specs=[pl.BlockSpec(memory_space=pltpu.VMEM)] * 4,
+        out_specs=(pl.BlockSpec(memory_space=pltpu.VMEM),) * 2,
+        scratch_shapes=[
+            pltpu.VMEM((4, 8, 16, 128), b16),
+            pltpu.VMEM((4, 8, 4, 16, 128), b16),
+            pltpu.VMEM((3, 16, 128), b16),
+            pltpu.VMEM((4, 8, 16, 128), b16),
+            pltpu.VMEM((4, 8, 128), jnp.float32),
+            pltpu.VMEM((8, 8, 128), jnp.float32),
+            pltpu.VMEM((4, 4, 8, 16, 128), b16),
+            sem((2,)),
+            sem((4,)), sem((4,)), sem((8,)), sem((8,)), sem((4,)), sem((4,)),
+            sem((4,)), sem((4,)), sem((8,)), sem((8,)), sem((4,)), sem((4,)),
+            sem((4,)), sem((4,)), sem((8,)), sem((8,)), sem((8,)), sem((8,)),
+            sem((4,)), sem((4,)), sem((4, 4)), sem((4, 4)),
+        ],
+        compiler_params=pltpu.CompilerParams(collective_id=0, has_side_effects=True),
+    )(w, pt, cnt, bias)
+    gp = jnp.transpose(gp, (1, 0, 2))[:, ::-1].reshape(16, 64)
+    gp = lax.dynamic_slice_in_dim(
+        jnp.concatenate([gp, gp], axis=1), (3 + NY - y) % NY * 16, 64, 1
+    )
+    return loss[0, 0], gp
 
 
 def split_length(padded_len):
@@ -128,24 +356,7 @@
     mixed = conv + skip_gain[:, None] * key_value
     output = query * mixed
     pooled = output.reshape(channels, bins, POOL).mean(axis=2).astype(jnp.bfloat16)
-    partial_value = jnp.einsum("cb,ct->bt", pooled, head_weight, preferred_element_type=jnp.float32)
-    logits = lax.psum(partial_value, "chan") + head_bias[None, :]
-    rates = jax.nn.softplus(logits) + rate_floor
-    observed = counts.astype(jnp.float32)
-    local_log = jnp.sum(observed * jnp.log(rates))
-    pred_total, obs_total, log_sum = lax.psum(
-        (jnp.sum(rates, axis=0), jnp.sum(observed, axis=0), local_log), "seq"
-    )
-    log_pred = jnp.log(pred_total)
-    loss_sum = (
-        jnp.sum(total_weight * (pred_total - obs_total * log_pred) + obs_total * log_pred) - log_sum
-    )
-    ratio = obs_total / pred_total
-    grad_rates = total_weight * (1.0 - ratio)[None, :] + ratio[None, :] - observed / rates
-    grad_logits = (grad_rates * jax.nn.sigmoid(logits)).astype(jnp.bfloat16)
-    grad_pooled = jnp.einsum(
-        "bt,ct->cb", grad_logits, head_weight, preferred_element_type=jnp.float32
-    )
+    loss_sum, grad_pooled = head(pooled, head_weight, head_bias, counts)
     mean_loss = loss_sum / (bins * seq_count * tracks)
     grad_output = jnp.broadcast_to(grad_pooled[:, :, None] / POOL, (channels, bins, POOL)).reshape(
         channels, width

time: 640 us -> 173 us (0.27)
  waiting for transfers between devices: 501 us -> 9.05 us
  Pallas kernels: 0 us -> 81.1 us
  blocking collectives: 55 us -> 10.6 us
  between operations: 16.9 us -> 2.9 us
  local copies, waits for them, and re-layouts: 6.16 us -> 13.6 us
    psum x1 -> x0, waiting for transfers between devices: 486 us -> none  [per_device(): logits = lax.psum(partial_value, 'chan') + head_bias[None, :]]
    pallas_call x0 -> x1, Pallas kernels: none -> 81.1 us  [head(): pl.pallas_call(head_kernel, out_shape=(jax.ShapeDtypeStruct((NY, 16, 16),...]
    psum x1 -> x0, blocking collectives: 44.2 us -> none  [per_device(): lax.psum((jnp.sum(rates, axis=0), jnp.sum(observed, axis=0), local_log),...]
  transfers between devices with their start and end apart: 4 -> 3, of which waited for: 4 -> 3; matrix products, arithmetic and copies ran while one was open for 0% -> 3% of each run, Pallas kernels for 0% -> 0%
where the time goes in v1:
time: 173 us; the launch traced here: 172 us
  Pallas kernels  81.1 us (47%)
  starting transfers between devices  25.9 us (15%)
  matrix products  24.9 us (14%)
  local copies, waits for them, and re-layouts  13.6 us (8%)
  blocking collectives  10.6 us (6%)
  waiting for transfers between devices  9.05 us (5%)
  other arithmetic  4.52 us (3%)
  between operations  2.9 us (2%)
    pallas_call x1, Pallas kernels, head(): pl.pallas_call(head_kernel, out_shape=(jax.ShapeDtypeStruct((NY, 16, 16),...  81.1 us
    all_to_all x1, starting transfers between devices, to_pencil(): lax.all_to_all(stacked, 'seq', split_axis=1, concat_axis=2, tiled=True)  17.4 us
    all_to_all x1, blocking collectives, to_pencil(): lax.all_to_all(stacked, 'seq', split_axis=1, concat_axis=2, tiled=True)  10.6 us
    all_to_all x2, starting transfers between devices, from_pencil(): lax.all_to_all(pencil_rows, 'seq', split_axis=1, concat_axis=0, tiled=True)  8.47 us
    all_to_all x2, waiting for transfers between devices, from_pencil(): lax.all_to_all(pencil_rows, 'seq', split_axis=1, concat_axis=0, tiled=True)  7.81 us
  transfers between devices with their start and end apart: 3, of which 3 were waited for; matrix products, arithmetic and copies ran while one was open for 3% of the time, Pallas kernels for 0%

profile of v1, /device:TPU:1, one launch (start us, length us, event | category | flops | bytes accessed | tf_op | source)
XLA Modules:
  0.0 172.4 jit_solution(6367362617742426903)
XLA Ops:
  0.6 0.9 convert_multiply_fusion.1
  1.6 0.9 copy.73
  2.5 17.4 %all-to-all-start = ((f32[2,16,2048]{2,0,1:T(2,128)}), f32[2,16,2048]{2,0,1:T(2,128)S(1)}, u32[]{:S(2)}, u32[]{:S(2)}) async-start(f32[2,16,2048]{2,0,1:T(2,128)} %copy.73), calls=%async_computation | async-start | bytes 524288 | tf_op jit(solution)/shard_map/all_to_all | solution.py:318
  20.1 0.8 copy-done
  21.9 0.7 copy-done.2
  23.0 0.8 dynamic_slice.17
  24.4 0.8 dynamic_slice.18
  25.2 1.2 all-to-all-done
  27.5 1.8 %convolution_bitcast_fusion = f32[4,256,128]{1,2,0:T(8,128)S(1)} fusion(f32[4,256,128]{2,1,0:T(8,128)S(1)} %reshape.127), kind=kOutput, calls=%fused_computation | convolution fusion | flops 403636224 | bytes 1048576 | tf_op jit(solution)/shard_map/ka,mab->mkb/dot_general | solution.py:288
  29.3 1.8 %convolution_bitcast_fusion.1 = f32[4,256,128]{1,2,0:T(8,128)S(1)} fusion(f32[4,256,128]{2,1,0:T(8,128)S(1)} %reshape.127), kind=kOutput, calls=%fused_computation.1 | convolution fusion | flops 403570688 | bytes 1048576 | tf_op jit(solution)/shard_map/ka,mab->mkb/dot_general | solution.py:287
  31.1 1.2 fusion.85
  32.3 1.2 fusion.70
  33.5 1.2 convolution_subtract_fusion
  34.8 1.2 convolution_add_fusion
  36.7 0.8 fusion.80
  38.7 1.5 fusion.16
  40.3 1.5 fusion.3
  42.8 4.3 %all-to-all-start.1 = ((f32[2,8,2048]{2,0,1:T(2,128)}), f32[2,8,2048]{2,0,1:T(2,128)S(1)}, u32[]{:S(2)}, u32[]{:S(2)}) async-start(f32[2,8,2048]{2,0,1:T(2,128)} %bitcast.12), calls=%async_computation.1 | async-start | bytes 262144 | tf_op jit(solution)/shard_map/all_to_all | solution.py:322
  47.1 0.9 fusion.39
  48.0 4.4 %all-to-all-done.1 = f32[2,8,2048]{2,0,1:T(2,128)S(1)} async-done(((f32[2,8,2048]{2,0,1:T(2,128)}), f32[2,8,2048]{2,0,1:T(2,128)S(1)}, u32[]{:S(2)}, u32[]{:S(2)}) %all-to-all-start.1) | async-done | bytes 131104 | tf_op jit(solution)/shard_map/all_to_all | solution.py:322
  55.6 81.1 %shard_map.77 = (f32[4,16,16]{2,1,0:T(8,128)}, f32[8,128]{1,0:T(8,128)}) custom-call(bf16[8,4,16,128]{3,2,1,0:T(8,128)(2,1)} %bitcast.129, bf16[4,16,128]{2,1,0:T(8,128)(2,1)} %pad_maximum_fusion.2.p_ref, s32[16,128]{1,0:T(8,128)} %pad.35.cnt_ref, f32[8,128]{1,0:T(8,128)} %broadcast_in_dim.4.bias_ref), custom_call_target="tpu_custom_call" | custom-call | tf_op jit(solution)/shard_map/pallas_call | solution.py:212
  136.7 0.8 rev.3
  138.3 10.6 %all_to_all.77 = f32[1,16,2048]{2,0,1:T(1,128)S(1)} all-to-all(f32[1,16,2048]{2,0,1:T(1,128)S(1)} %copy.89), channel_id=1, replica_groups=mesh['seq'=8,'chan'=128] {'seq'}, dimensions={1} | all-to-all | bytes 262144 | tf_op jit(solution)/shard_map/all_to_all | solution.py:318
  149.1 1.4 convolution_bitcast_fusion.2
  150.5 1.4 convolution_bitcast_fusion.3
  153.7 0.7 multiply_add_fusion.1
  156.9 1.5 fusion.13
  158.4 1.5 fusion.1
  160.9 4.2 %all-to-all-start.3 = ((f32[2,8,2048]{2,0,1:T(2,128)}), f32[2,8,2048]{2,0,1:T(2,128)S(1)}, u32[]{:S(2)}, u32[]{:S(2)}) async-start(f32[2,8,2048]{2,0,1:T(2,128)} %bitcast.26), calls=%async_computation.3 | async-start | bytes 262144 | tf_op jit(solution)/shard_map/all_to_all | solution.py:322
  165.1 1.2 slice.58
  166.9 3.4 %all-to-all-done.3 = f32[2,8,2048]{2,0,1:T(2,128)S(1)} async-done(((f32[2,8,2048]{2,0,1:T(2,128)}), f32[2,8,2048]{2,0,1:T(2,128)S(1)}, u32[]{:S(2)}, u32[]{:S(2)}) %all-to-all-start.3) | async-done | bytes 131104 | tf_op jit(solution)/shard_map/all_to_all | solution.py:322
  170.5 0.8 pad_maximum_fusion
  (67 shorter events, 15.7 us)
Async XLA Ops:
  0.6 1.0 copy-start.1
  2.5 23.9 %all-to-all-start = ((f32[2,16,2048]{2,0,1:T(2,128)}), f32[2,16,2048]{2,0,1:T(2,128)S(1)}, u32[]{:S(2)}, u32[]{:S(2)}) async-start(f32[2,16,2048]{2,0,1:T(2,128)} %copy.73), calls=%async_computation | async-start | bytes 524288 | tf_op jit(solution)/shard_map/all_to_all | solution.py:318
  20.0 0.9 copy-start
  21.7 0.9 copy-start.2
  42.8 9.6 %all-to-all-start.1 = ((f32[2,8,2048]{2,0,1:T(2,128)}), f32[2,8,2048]{2,0,1:T(2,128)S(1)}, u32[]{:S(2)}, u32[]{:S(2)}) async-start(f32[2,8,2048]{2,0,1:T(2,128)} %bitcast.12), calls=%async_computation.1 | async-start | bytes 262144 | tf_op jit(solution)/shard_map/all_to_all | solution.py:322
  52.6 0.7 copy-start.3
  160.9 9.4 %all-to-all-start.3 = ((f32[2,8,2048]{2,0,1:T(2,128)}), f32[2,8,2048]{2,0,1:T(2,128)S(1)}, u32[]{:S(2)}, u32[]{:S(2)}) async-start(f32[2,8,2048]{2,0,1:T(2,128)} %bitcast.26), calls=%async_computation.3 | async-start | bytes 262144 | tf_op jit(solution)/shard_map/all_to_all | solution.py:322

commit v2 on v1

v2 whole, which is shorter than its diff:
```python
import jax
import jax.numpy as jnp
from jax import lax
from jax.experimental import pallas as pl
from jax.experimental.pallas import tpu as pltpu
from jax.sharding import PartitionSpec as P

POOL = 32
NY = 4
NZ = 32
NS = 8
TR = 120
MESH = pl.DeviceIdType.MESH

total_weight = 0.2
rate_floor = 0.5


def step_kernel(
    x_ref, h_ref, skip_ref, w_ref, cnt_ref, bias_ref,
    out_ref, loss_ref,
    kv, hx, rx, xp, hf, sh, tt, yy, cv, oo, gx, gg_out, gr, pp,
    wa, wg, py, pg, ty, ts, gg,
    s_loc, s_kv, r_kv, s_hx, r_hx, s_cv, r_cv, s_gx, r_gx, s_gr, r_gr,
    s_wa, r_wa, s_wb, r_wb, s_wy, r_wy, s_py, r_py, s_pf, r_pf, s_pn, r_pn,
    s_ty, r_ty, s_ts, r_ts, s_gf, r_gf, s_gn, r_gn, s_gy, r_gy,
):
    s = lax.axis_index("seq")
    ch = lax.axis_index("chan")
    y = ch // NZ
    z = ch % NZ

    def zdev(d):
        return (s, y * NZ + (z + d + NZ) % NZ)

    def ydev(d):
        return (s, ((y + d) % NY) * NZ + z)

    def sdev(d):
        return ((s + d) % NS, ch)

    def send(src, dst, ss, rs, dev):
        c = pltpu.make_async_remote_copy(
            src_ref=src, dst_ref=dst, send_sem=ss, recv_sem=rs, device_id=dev, device_id_type=MESH
        )
        c.start()
        return c

    near = ((0, -1), (2, 1), (3, 2))

    barrier = pltpu.get_barrier_semaphore()
    peers = [sdev(d) for d in range(1, NS)] + [ydev(d) for d in range(1, NY)]
    peers += [zdev(4 * k) for k in range(1, 8)] + [zdev(d) for d in (-2, -1, 1, 2)]
    for dev in peers:
        pl.semaphore_signal(barrier, inc=1, device_id=dev, device_id_type=MESH)


    key_value = x_ref[1].astype(jnp.float32) * x_ref[2].astype(jnp.float32)
    kv[...] = key_value.astype(jnp.bfloat16).reshape(NS, 2, 16, 128)
    for c in range(2):
        xp[c, 0:16, :] = jnp.zeros((16, 128), jnp.float32)
        xp[c, 144:160, :] = jnp.zeros((16, 128), jnp.float32)
    pl.semaphore_wait(barrier, len(peers))

    c_hx = [
        send(h_ref.at[(s + d) % NS], hx.at[d - 1], s_hx.at[d], r_hx.at[d], sdev(d))
        for d in range(1, NS)
    ]
    c_kv = [
        send(kv.at[(s + d) % NS], rx.at[d], s_kv.at[d], r_kv.at[d], sdev(d)) for d in range(1, NS)
    ]
    c_wa = [send(w_ref.at[:, m], wa.at[m], s_wa.at[m], r_wa.at[m], zdev(o)) for m, o in near]
    own_wa = pltpu.make_async_copy(w_ref.at[:, 1], wa.at[1], s_loc.at[0])
    own_wa.start()
    for c in c_hx:
        c.wait_recv()

    def put_taps(d, block):
        a = pl.multiple_of((s + NS - d) % NS * 16, 16)
        for c in range(2):
            hf[c, pl.ds(a, 16), :] = block[c].astype(jnp.float32)

    put_taps(0, h_ref[s])
    for d in range(1, NS):
        put_taps(d, hx[d - 1])

    row = lax.broadcasted_iota(jnp.int32, (128, 128), 0)
    col = lax.broadcasted_iota(jnp.int32, (128, 128), 1)
    upper = col >= row

    def taps_blocks(c):
        def body(d, last):
            line = jnp.broadcast_to(hf[c, pl.ds(d, 1), :], (128, 128))
            now = pltpu.roll(line, 0, 1, stride=1, stride_axis=0)
            tt[c, d] = jnp.where(upper, now, last).astype(jnp.bfloat16)
            return now

        lax.fori_loop(0, 128, body, jnp.zeros((128, 128), jnp.float32), unroll=4)

    taps_blocks(0)
    own_wa.wait()
    for c in c_wa:
        c.wait_recv()
    c_wb = [
        send(wa.at[:, k], wg.at[0, k], s_wb.at[k], r_wb.at[k], zdev(4 * k)) for k in range(1, 8)
    ]
    own_wb = pltpu.make_async_copy(wa.at[:, 0], wg.at[0, 0], s_loc.at[1])
    own_wb.start()
    taps_blocks(1)

    def place(blocks):
        for a in range(NS):
            for c in range(2):
                xp[c, 16 + 16 * a : 32 + 16 * a, :] = blocks[(s + NS - a) % NS, c].astype(
                    jnp.float32
                )

    for c in c_kv:
        c.wait_recv()
    rx[0] = kv[s]
    place(rx)

    def forward(c, carry):
        for d in range(16):
            sh[:, 128 * d : 128 * d + 128] = xp[c, 16 - d : 144 - d, :].astype(jnp.bfloat16)
        for p in range(4):
            taps = jnp.concatenate(
                [tt[c, 32 * p + 16 * h : 32 * p + 16 * h + 16].reshape(2048, 128) for h in range(2)],
                axis=1,
            )
            rows = 128 - 32 * p
            part = jnp.dot(sh[0:rows, :], taps, preferred_element_type=jnp.float32)
            first = part[:, :128].reshape(8 - 2 * p, 16, 128)
            second = part[: rows - 16, 128:].reshape(7 - 2 * p, 16, 128)
            if p == 0:
                yy[c] = first
            else:
                yy[c, 2 * p : 8] = yy[c, 2 * p : 8] + first
            yy[c, 2 * p + 1 : 8] = yy[c, 2 * p + 1 : 8] + second
        return carry

    lax.fori_loop(0, 2, forward, 0)
    c_cv = [
        send(yy.at[:, (s + d) % NS], cv.at[d], s_cv.at[d], r_cv.at[d], sdev(d))
        for d in range(1, NS)
    ]
    cv[0] = yy[:, s]
    own_wb.wait()
    for c in c_wb:
        c.wait_recv()
    c_wy = [
        send(wg.at[0], wg.at[d], s_wy.at[d], r_wy.at[d], ydev(d)) for d in range(1, NY)
    ]
    for c in c_cv:
        c.wait_recv()

    def collect(blocks):
        return jnp.concatenate(
            [blocks[(s + NS - a) % NS].reshape(32, 128) for a in range(NS)], axis=0
        )

    skip = skip_ref[...]
    query = x_ref[0].astype(jnp.float32)
    mixed = collect(cv) + skip * key_value
    oo[...] = query * mixed
    out_ref[0] = mixed

    small_row = lax.broadcasted_iota(jnp.int32, (16, 128), 0)
    small_col = lax.broadcasted_iota(jnp.int32, (16, 128), 1)
    spread = [
        jnp.where(
            (small_row // 4 == j) & (small_col // 32 == small_row % 4), 1.0 / POOL, 0.0
        ).astype(jnp.bfloat16)
        for j in range(4)
    ]

    def halves(val):
        top = val.astype(jnp.bfloat16)
        return top, (val - top.astype(jnp.float32)).astype(jnp.bfloat16)

    nt = (((1,), (1,)), ((), ()))
    nn = (((1,), (0,)), ((), ()))
    for d in range(NY):
        mean = jnp.zeros((16, 16), jnp.float32)
        for j in range(4):
            rows = oo[pl.ds((y + d) % NY * 4 + j, 16, stride=16), :]
            for piece in halves(rows):
                mean = mean + lax.dot_general(
                    spread[j], piece, nt, preferred_element_type=jnp.float32
                )
        lanes_of = (small_col == small_row + 16 * d).astype(jnp.float32).astype(jnp.bfloat16)
        pp[d] = lax.dot_general(
            mean.astype(jnp.bfloat16), lanes_of, nn, preferred_element_type=jnp.float32
        ).astype(jnp.bfloat16)
    c_py = [
        send(pp.at[d], py.at[d - 1], s_py.at[d], r_py.at[d], ydev(d)) for d in range(1, NY)
    ]
    for c in c_py:
        c.wait_recv()
    tile = pp[0].astype(jnp.float32)
    for d in range(NY - 1):
        tile = tile + py[d].astype(jnp.float32)
    pg[1, 0] = tile.astype(jnp.bfloat16)
    c_pf = [
        send(pg.at[1, 0], pg.at[1, k], s_pf.at[k], r_pf.at[k], zdev(4 * k)) for k in range(1, 8)
    ]
    for c in c_pf:
        c.wait_recv()
    c_pn = [send(pg.at[1], pg.at[m], s_pn.at[m], r_pn.at[m], zdev(o)) for m, o in near]

    for c in c_pn:
        c.wait_recv()
    for c in c_wy:
        c.wait_recv()

    logits = jnp.broadcast_to(bias_ref[0:1, :], (16, 128))
    for k in range(8):
        for m in range(4):
            rows = jnp.concatenate([wg[d, k, m] for d in range(NY)], axis=0)
            logits = logits + lax.dot_general(
                pg[m, k][:, :64], rows, (((1,), (0,)), ((), ())),
                preferred_element_type=jnp.float32,
            )
    rates = jnp.maximum(logits, 0.0) + jnp.log1p(jnp.exp(-jnp.abs(logits))) + rate_floor
    observed = cnt_ref[...].astype(jnp.float32)
    part = [
        jnp.sum(rates, axis=0, keepdims=True),
        jnp.sum(observed, axis=0, keepdims=True),
        jnp.sum(observed * jnp.log(rates), axis=0, keepdims=True),
        jnp.zeros((5, 128), jnp.float32),
    ]
    ty[0] = jnp.concatenate(part, axis=0)
    c_ty = [send(ty.at[0], ty.at[d], s_ty.at[d], r_ty.at[d], ydev(d)) for d in range(1, NY)]
    sig = 1.0 / (1.0 + jnp.exp(-logits))
    obs_rate = observed / rates
    for c in c_ty:
        c.wait_recv()
    tot = ty[y]
    for a in range(1, NY):
        tot = tot + ty[(y + NY - a) % NY]
    ts[0] = tot
    c_ts = [send(ts.at[0], ts.at[d], s_ts.at[d], r_ts.at[d], sdev(d)) for d in range(1, NS)]
    for c in c_ts:
        c.wait_recv()
    tot = ts[s]
    for a in range(1, NS):
        tot = tot + ts[(s + NS - a) % NS]
    pred = tot[0:1, :]
    obs = tot[1:2, :]
    log_pred = jnp.log(pred)
    lane = lax.broadcasted_iota(jnp.int32, (1, 128), 1)
    terms = total_weight * (pred - obs * log_pred) + obs * log_pred - tot[2:3, :]
    loss = jnp.sum(jnp.where(lane < TR, terms, 0.0), axis=1, keepdims=True)
    ratio = obs / pred
    grad_rates = total_weight * (1.0 - ratio) + ratio - obs_rate
    grad = grad_rates * sig
    hi = loss.astype(jnp.bfloat16).astype(jnp.float32)
    mid = (loss - hi).astype(jnp.bfloat16).astype(jnp.float32)
    lo = loss - hi - mid
    lanes = lax.broadcasted_iota(jnp.int32, (16, 128), 1)
    grad = jnp.where(
        lanes < TR, grad, jnp.where(lanes == TR, hi, jnp.where(lanes == TR + 1, mid, lo))
    )
    gg[0, 1, 0] = grad.astype(jnp.bfloat16)
    c_gf = [
        send(gg.at[0, 1, 0], gg.at[0, 1, k], s_gf.at[k], r_gf.at[k], zdev(-4 * k))
        for k in range(1, 8)
    ]
    for c in c_gf:
        c.wait_recv()
    c_gn = [
        send(gg.at[0, 1], gg.at[0, m], s_gn.at[m], r_gn.at[m], zdev(-o)) for m, o in near
    ]
    c_gy = [
        send(gg.at[0, 1], gg.at[d, 1], s_gy.at[d, 1], r_gy.at[d, 1], ydev(d))
        for d in range(1, NY)
    ]
    for c, (m, o) in zip(c_gn, near):
        c.wait_recv()
        c_gy += [
            send(gg.at[0, m], gg.at[d, m], s_gy.at[d, m], r_gy.at[d, m], ydev(d))
            for d in range(1, NY)
        ]

    by_z = jnp.zeros((1, 128), jnp.float32)
    for k in range(8):
        for m in range(4):
            row = gg[0, m, k][0:1, :].astype(jnp.float32)
            val = jnp.sum(
                jnp.where((lane >= TR) & (lane < TR + 3), row, 0.0), axis=1, keepdims=True
            )
            by_z = jnp.where(lane == (z + m - 1 + 4 * k + NZ) % NZ, val, by_z)
    loss_ref[...] = jnp.broadcast_to(jnp.sum(by_z, axis=1, keepdims=True), (8, 128))


    wl = jnp.concatenate([w_ref[k, m] for k in range(8) for m in range(4)], axis=1)

    def grad_block(d):
        gl = jnp.concatenate([gg[d, m, k] for k in range(8) for m in range(4)], axis=1)
        block = lax.dot_general(wl, gl, nt, preferred_element_type=jnp.float32)
        top, low = halves(block)
        for j in range(4):
            rows = lax.dot_general(top, spread[j], nn, preferred_element_type=jnp.float32)
            rows = rows + lax.dot_general(low, spread[j], nn, preferred_element_type=jnp.float32)
            oo[pl.ds((y + NY - d) % NY * 4 + j, 16, stride=16), :] = rows

    grad_block(0)
    for c in c_gy:
        c.wait_recv()
    for d in range(1, NY):
        grad_block(d)

    gated = oo[...] * query
    gg_out[...] = gated.astype(jnp.bfloat16).reshape(NS, 2, 16, 128)
    c_gx = [
        send(gg_out.at[(s + d) % NS], gx.at[d], s_gx.at[d], r_gx.at[d], sdev(d))
        for d in range(1, NS)
    ]
    gx[0] = gg_out[s]
    out_ref[0] = oo[...] * out_ref[0]
    for c in c_cv:
        c.wait_send()
    for c in c_gx:
        c.wait_recv()
    place(gx)

    def backward(c, carry):
        for d in range(16):
            sh[:, 128 * d : 128 * d + 128] = xp[c, 16 + d : 144 + d, :].astype(jnp.bfloat16)
        for p in range(4):
            taps = jnp.concatenate(
                [
                    jnp.concatenate([tt[c, 32 * p + 16 * h + e] for e in range(16)], axis=1)
                    for h in range(2)
                ],
                axis=0,
            )
            rows = 128 - 32 * p
            part = lax.dot_general(
                sh[32 * p : 128, :], taps, nt, preferred_element_type=jnp.float32
            )
            first = part[:, :128].reshape(8 - 2 * p, 16, 128)
            second = part[16:, 128:].reshape(7 - 2 * p, 16, 128)
            if p == 0:
                yy[c] = first
            else:
                yy[c, 0 : 8 - 2 * p] = yy[c, 0 : 8 - 2 * p] + first
            yy[c, 0 : 7 - 2 * p] = yy[c, 0 : 7 - 2 * p] + second
        return carry

    lax.fori_loop(0, 2, backward, 0)
    c_gr = [
        send(yy.at[:, (s + d) % NS], gr.at[d], s_gr.at[d], r_gr.at[d], sdev(d))
        for d in range(1, NS)
    ]
    gr[0] = yy[:, s]
    for c in c_gr:
        c.wait_recv()
    grad_kv = collect(gr) + skip * (oo[...] * query)
    out_ref[1] = grad_kv * x_ref[2].astype(jnp.float32)
    out_ref[2] = grad_kv * x_ref[1].astype(jnp.float32)

    for c in c_hx + c_kv + c_wa + c_py + c_wb + c_pf + c_pn + c_wy + c_ty + c_ts:
        c.wait_send()
    for c in c_gf + c_gn + c_gy + c_gx + c_gr:
        c.wait_send()


def per_device(projections, filter_taps, skip_gain, head_weight, head_bias, counts):
    ch = lax.axis_index("chan")
    y = ch // NZ
    z = ch % NZ
    x = projections.reshape(3, 256, 128)
    h = filter_taps.astype(jnp.bfloat16).reshape(NS, 2, 16, 128)
    skip = jnp.broadcast_to(skip_gain[:, None], (16, 16)).reshape(256, 1)
    w = jnp.pad(head_weight.reshape(16, NZ, TR), ((0, 0), (0, 0), (0, 128 - TR)))
    w = jnp.transpose(w, (1, 0, 2))
    w = lax.dynamic_slice_in_dim(jnp.concatenate([w, w], axis=0), (z + NZ - 1) % NZ, NZ, 0)
    w = w.reshape(8, 4, 16, 128)
    cnt = lax.dynamic_slice(counts, (y * 16, z * TR), (16, TR))
    cnt = jnp.pad(cnt, ((0, 0), (0, 128 - TR)))
    bias = jnp.pad(lax.dynamic_slice_in_dim(head_bias, z * TR, TR, 0), (0, 128 - TR))
    bias = jnp.broadcast_to(bias[None, :], (8, 128))
    sem = pltpu.SemaphoreType.DMA
    b16 = jnp.bfloat16
    f32 = jnp.float32
    out, loss = pl.pallas_call(
        step_kernel,
        out_shape=(
            jax.ShapeDtypeStruct((3, 256, 128), f32),
            jax.ShapeDtypeStruct((8, 128), f32),
        ),
        in_specs=[pl.BlockSpec(memory_space=pltpu.VMEM)] * 6,
        out_specs=(pl.BlockSpec(memory_space=pltpu.VMEM),) * 2,
        scratch_shapes=[
            pltpu.VMEM((8, 2, 16, 128), b16),
            pltpu.VMEM((7, 2, 16, 128), b16),
            pltpu.VMEM((8, 2, 16, 128), b16),
            pltpu.VMEM((2, 160, 128), f32),
            pltpu.VMEM((2, 128, 128), f32),
            pltpu.VMEM((128, 2048), b16),
            pltpu.VMEM((2, 128, 128, 128), b16),
            pltpu.VMEM((2, 8, 16, 128), f32),
            pltpu.VMEM((8, 2, 16, 128), f32),
            pltpu.VMEM((256, 128), f32),
            pltpu.VMEM((8, 2, 16, 128), b16),
            pltpu.VMEM((8, 2, 16, 128), b16),
            pltpu.VMEM((8, 2, 16, 128), f32),
            pltpu.VMEM((4, 16, 128), b16),
            pltpu.VMEM((4, 8, 16, 128), b16),
            pltpu.VMEM((4, 8, 4, 16, 128), b16),
            pltpu.VMEM((3, 16, 128), b16),
            pltpu.VMEM((4, 8, 16, 128), b16),
            pltpu.VMEM((4, 8, 128), f32),
            pltpu.VMEM((8, 8, 128), f32),
            pltpu.VMEM((4, 4, 8, 16, 128), b16),
            sem((2,)),
            sem((8,)), sem((8,)), sem((8,)), sem((8,)), sem((8,)), sem((8,)),
            sem((8,)), sem((8,)), sem((8,)), sem((8,)),
            sem((4,)), sem((4,)), sem((8,)), sem((8,)), sem((4,)), sem((4,)),
            sem((4,)), sem((4,)), sem((8,)), sem((8,)), sem((4,)), sem((4,)),
            sem((4,)), sem((4,)), sem((8,)), sem((8,)), sem((8,)), sem((8,)),
            sem((4,)), sem((4,)), sem((4, 4)), sem((4, 4)),
        ],
        compiler_params=pltpu.CompilerParams(collective_id=0, has_side_effects=True),
    )(x, h, skip, w, cnt, bias)
    mean_loss = loss[0, 0] / (512 * 3840)
    return mean_loss, out.reshape(3, 16, 2048)


def solution(mesh):
    placed = (
        P(None, "chan", "seq"),
        P("chan", "seq"),
        P("chan"),
        P("chan", None),
        P(),
        P("seq", None),
    )
    return jax.shard_map(
        per_device,
        mesh=mesh,
        in_specs=placed,
        out_specs=(P(), P(None, "chan", "seq")),
        check_vma=False,
    )
```

time: 173 us -> 134 us (0.77)
  Pallas kernels: 81.1 us -> 121 us
  starting transfers between devices: 25.9 us -> 0 us
  matrix products: 24.9 us -> 0 us
  blocking collectives: 10.6 us -> 0 us
  waiting for transfers between devices: 9.05 us -> 0 us
  local copies, waits for them, and re-layouts: 13.6 us -> 9.07 us
  other arithmetic: 4.52 us -> 0.9 us
    pallas_call x1, Pallas kernels: 81.1 us -> 121 us  [per_device(): pl.pallas_call(step_kernel, out_shape=(jax.ShapeDtypeStruct((3, 256, 128)...]
    all_to_all x3 -> x0, starting transfers between devices: 25.9 us -> none  [the longest x1 17.4 us: to_pencil(): lax.all_to_all(stacked, 'seq', split_axis=1, concat_axis=2, tiled=True)]
    dot_general x24 -> x0, matrix products: 24.9 us -> none  [the longest x2 3.18 us: forward(): first_im = jnp.einsum('ka,mab->mkb', outer_im, real_in, precision=highest)]
    all_to_all x1 -> x0, blocking collectives: 10.6 us -> none  [to_pencil(): lax.all_to_all(stacked, 'seq', split_axis=1, concat_axis=2, tiled=True)]
    all_to_all x3 -> x0, waiting for transfers between devices: 9.05 us -> none  [the longest x2 7.81 us: from_pencil(): lax.all_to_all(pencil_rows, 'seq', split_axis=1, concat_axis=0, tiled=True)]
    reshape x5, local copies, waits for them, and re-layouts: 1.14 us -> 3.69 us  [the longest x1 1.81 us: per_device(): return (mean_loss, out.reshape(3, 16, 2048))]
    unnamed x15 -> x7, local copies, waits for them, and re-layouts: 2.86 us -> 0.67 us
  transfers between devices with their start and end apart: 3 -> 0, of which waited for: 3 -> 0; matrix products, arithmetic and copies ran while one was open for 3% -> 0% of each run, Pallas kernels for 0% -> 0%
where the time goes in v2:
time: 134 us
  Pallas kernels  121 us (90%)
  local copies, waits for them, and re-layouts  9.07 us (7%)
  between operations  2.52 us (2%)
    pallas_call x1, Pallas kernels, per_device(): pl.pallas_call(step_kernel, out_shape=(jax.ShapeDtypeStruct((3, 256, 128)...  121 us

profile of v2, /device:TPU:1, one launch (start us, length us, event | category | flops | bytes accessed | tf_op | source)
XLA Modules:
  0.0 133.7 jit_solution(6446441568980094755)
XLA Ops:
  0.6 0.0 copy-start.1
  0.7 0.8 dynamic_slice.11
  1.5 0.6 broadcast_in_dim.5.bias_ref
  2.1 0.8 dynamic_slice.10
  2.9 0.6 pad.13.cnt_ref
  3.4 0.7 broadcast_in_dim.4
  4.2 0.0 copy-done.1
  4.2 0.0 copy-start.2
  4.2 0.6 copy.11
  4.8 0.7 reshape.32.skip_ref
  5.6 0.0 copy-done.2
  5.6 0.3 reshape.29
  5.9 0.1 copy.9
  6.0 0.0 copy-start
  6.0 0.9 fusion
  6.9 0.0 copy-done
  6.9 0.8 reshape.26.x_ref
  7.7 121.2 %shard_map.77 = (f32[3,256,128]{2,1,0:T(8,128)}, f32[8,128]{1,0:T(8,128)}) custom-call(bf16[3,256,128]{2,1,0:T(8,128)(2,1)} %reshape.26.x_ref, bf16[8,2,16,128]{3,2,1,0:T(8,128)(2,1)} %bitcast.9, f32[256,1]{1,0:T(8,128)} %reshape.32.skip_ref, bf16[8,4,16,128]{3,2,1,0:T(8,128)(2,1)} %bitcast.8, s32[16,128]{1,0:T(8,128)} %pad.13.cnt_ref, ...), custom_call_target="tpu_custom_call" | custom-call | tf_op jit(solution)/shard_map/pallas_call | solution.py:387
  128.9 1.2 slice.3
  130.8 1.8 %reshape.31 = f32[3,16,2048]{2,1,0:T(8,128)} reshape(f32[3,256,128]{2,1,0:T(8,128)} %get-tuple-element.5) | data formatting | bytes 786432 | tf_op jit(solution)/shard_map/reshape | solution.py:428
  (3 shorter events, 0.0 us)
Async XLA Ops:
  0.6 3.5 %copy-start.1 = (f32[16,2048]{1,0:T(8,128)S(1)}, f32[16,2048]{1,0:T(8,128)}, u32[]{:S(2)}) copy-start(f32[16,2048]{1,0:T(8,128)} %param.7) | copy-start | bytes 393220
  4.2 1.4 %copy-start.2 = (bf16[16,3840]{1,0:T(8,128)(2,1)S(1)}, bf16[16,3840]{1,0:T(8,128)(2,1)}, u32[]{:S(2)}) copy-start(bf16[16,3840]{1,0:T(8,128)(2,1)} %param.9) | copy-start | bytes 368644
  6.0 0.9 copy-start

commit v3 on v2

--- a/solution.py
+++ b/solution.py
@@ -10,6 +10,8 @@
 NZ = 32
 NS = 8
 TR = 120
+FAR = (0, 1, 7, 2, 6, 3, 5, 4)
+GROUPS = ((0, 3), (3, 2), (5, 2), (7, 1))
 MESH = pl.DeviceIdType.MESH
 
 total_weight = 0.2
@@ -19,7 +21,7 @@
 def step_kernel(
     x_ref, h_ref, skip_ref, w_ref, cnt_ref, bias_ref,
     out_ref, loss_ref,
-    kv, hx, rx, xp, hf, sh, tt, yy, cv, oo, gx, gg_out, gr, pp,
+    kv, hx, rx, xp, hf, vf, vb, pick, sh, tt, yy, yb, cv, oo, gx, gg_out, gr, pp,
     wa, wg, py, pg, ty, ts, gg,
     s_loc, s_kv, r_kv, s_hx, r_hx, s_cv, r_cv, s_gx, r_gx, s_gr, r_gr,
     s_wa, r_wa, s_wb, r_wb, s_wy, r_wy, s_py, r_py, s_pf, r_pf, s_pn, r_pn,
@@ -60,6 +62,13 @@
     for c in range(2):
         xp[c, 0:16, :] = jnp.zeros((16, 128), jnp.float32)
         xp[c, 144:160, :] = jnp.zeros((16, 128), jnp.float32)
+        vf[c, 0:8, :] = jnp.zeros((8, 128), jnp.float32)
+    tall = lax.broadcasted_iota(jnp.int32, (256, 256), 0)
+    wide = lax.broadcasted_iota(jnp.int32, (256, 256), 1)
+    for q in range(8):
+        pick[q] = jnp.where(
+            tall == 128 + wide % 128 - 16 * q - 8 * (wide // 128), 1.0, 0.0
+        ).astype(jnp.bfloat16)
     pl.semaphore_wait(barrier, len(peers))
 
     c_hx = [
@@ -75,6 +84,16 @@
     for c in c_hx:
         c.wait_recv()
 
+    own_wa.wait()
+    for c in c_wa:
+        c.wait_recv()
+    c_wb = [
+        send(wa.at[:, FAR[e]], wg.at[0, e], s_wb.at[e], r_wb.at[e], zdev(4 * FAR[e]))
+        for e in range(7, 0, -1)
+    ][::-1]
+    own_wb = pltpu.make_async_copy(wa.at[:, 0], wg.at[0, 0], s_loc.at[1])
+    own_wb.start()
+
     def put_taps(d, block):
         a = pl.multiple_of((s + NS - d) % NS * 16, 16)
         for c in range(2):
@@ -84,29 +103,35 @@
     for d in range(1, NS):
         put_taps(d, hx[d - 1])
 
-    row = lax.broadcasted_iota(jnp.int32, (128, 128), 0)
-    col = lax.broadcasted_iota(jnp.int32, (128, 128), 1)
-    upper = col >= row
-
-    def taps_blocks(c):
+    lane8 = lax.broadcasted_iota(jnp.int32, (8, 128), 1)
+    sub8 = lax.broadcasted_iota(jnp.int32, (8, 128), 0)
+
+    def windows(c):
         def body(d, last):
-            line = jnp.broadcast_to(hf[c, pl.ds(d, 1), :], (128, 128))
+            line = jnp.broadcast_to(hf[c, pl.ds(d, 1), :], (8, 128))
             now = pltpu.roll(line, 0, 1, stride=1, stride_axis=0)
-            tt[c, d] = jnp.where(upper, now, last).astype(jnp.bfloat16)
+            vf[c, pl.ds(pl.multiple_of(8 + 8 * d, 8), 8), :] = jnp.where(
+                lane8 >= sub8, now, last
+            )
             return now
 
-        lax.fori_loop(0, 128, body, jnp.zeros((128, 128), jnp.float32), unroll=4)
-
-    taps_blocks(0)
-    own_wa.wait()
-    for c in c_wa:
-        c.wait_recv()
-    c_wb = [
-        send(wa.at[:, k], wg.at[0, k], s_wb.at[k], r_wb.at[k], zdev(4 * k)) for k in range(1, 8)
-    ]
-    own_wb = pltpu.make_async_copy(wa.at[:, 0], wg.at[0, 0], s_loc.at[1])
-    own_wb.start()
-    taps_blocks(1)
+        lax.fori_loop(0, 128, body, jnp.zeros((8, 128), jnp.float32), unroll=16)
+        vb[c, :, 0:128] = vf[c, 0:1024, :].astype(jnp.bfloat16)
+        vb[c, :, 128:256] = vf[c, 8:1032, :].astype(jnp.bfloat16)
+
+    windows(0)
+    windows(1)
+
+    def fill(q, carry):
+        for c in range(2):
+            block = jnp.dot(vb[c], pick[q], preferred_element_type=jnp.float32)
+            both = jnp.concatenate(
+                [block[:, :128].reshape(128, 8, 128), block[:, 128:].reshape(128, 8, 128)], axis=1
+            )
+            tt[c, :, pl.ds(pl.multiple_of(16 * q, 16), 16), :] = both.astype(jnp.bfloat16)
+        return carry
+
+    lax.fori_loop(0, 8, fill, 0)
 
     def place(blocks):
         for a in range(NS):
@@ -140,23 +165,18 @@
         return carry
 
     lax.fori_loop(0, 2, forward, 0)
+    yb[...] = yy[...].astype(jnp.bfloat16)
     c_cv = [
-        send(yy.at[:, (s + d) % NS], cv.at[d], s_cv.at[d], r_cv.at[d], sdev(d))
+        send(yb.at[:, (s + d) % NS], cv.at[d], s_cv.at[d], r_cv.at[d], sdev(d))
         for d in range(1, NS)
     ]
-    cv[0] = yy[:, s]
-    own_wb.wait()
-    for c in c_wb:
-        c.wait_recv()
-    c_wy = [
-        send(wg.at[0], wg.at[d], s_wy.at[d], r_wy.at[d], ydev(d)) for d in range(1, NY)
-    ]
+    cv[0] = yb[:, s]
     for c in c_cv:
         c.wait_recv()
 
     def collect(blocks):
         return jnp.concatenate(
-            [blocks[(s + NS - a) % NS].reshape(32, 128) for a in range(NS)], axis=0
+            [blocks[(s + NS - a) % NS].astype(jnp.float32).reshape(32, 128) for a in range(NS)], axis=0
         )
 
     skip = skip_ref[...]
@@ -202,12 +222,25 @@
         tile = tile + py[d].astype(jnp.float32)
     pg[1, 0] = tile.astype(jnp.bfloat16)
     c_pf = [
-        send(pg.at[1, 0], pg.at[1, k], s_pf.at[k], r_pf.at[k], zdev(4 * k)) for k in range(1, 8)
-    ]
-    for c in c_pf:
-        c.wait_recv()
-    c_pn = [send(pg.at[1], pg.at[m], s_pn.at[m], r_pn.at[m], zdev(o)) for m, o in near]
-
+        send(pg.at[1, 0], pg.at[1, e], s_pf.at[e], r_pf.at[e], zdev(4 * FAR[e]))
+        for e in range(7, 0, -1)
+    ][::-1]
+    own_wb.wait()
+    c_pn = []
+    c_wy = []
+    for g, (e, n) in enumerate(GROUPS):
+        for c in c_pf[max(e, 1) - 1 : e + n - 1]:
+            c.wait_recv()
+        c_pn += [
+            send(pg.at[1, e : e + n], pg.at[m, e : e + n], s_pn.at[m, g], r_pn.at[m, g], zdev(o))
+            for m, o in near
+        ]
+        for c in c_wb[max(e, 1) - 1 : e + n - 1]:
+            c.wait_recv()
+        c_wy += [
+            send(wg.at[0, e : e + n], wg.at[d, e : e + n], s_wy.at[d, g], r_wy.at[d, g], ydev(d))
+            for d in range(1, NY)
+        ]
     for c in c_pn:
         c.wait_recv()
     for c in c_wy:
@@ -263,24 +296,42 @@
     )
     gg[0, 1, 0] = grad.astype(jnp.bfloat16)
     c_gf = [
-        send(gg.at[0, 1, 0], gg.at[0, 1, k], s_gf.at[k], r_gf.at[k], zdev(-4 * k))
-        for k in range(1, 8)
-    ]
-    for c in c_gf:
-        c.wait_recv()
-    c_gn = [
-        send(gg.at[0, 1], gg.at[0, m], s_gn.at[m], r_gn.at[m], zdev(-o)) for m, o in near
-    ]
-    c_gy = [
-        send(gg.at[0, 1], gg.at[d, 1], s_gy.at[d, 1], r_gy.at[d, 1], ydev(d))
-        for d in range(1, NY)
-    ]
-    for c, (m, o) in zip(c_gn, near):
-        c.wait_recv()
-        c_gy += [
-            send(gg.at[0, m], gg.at[d, m], s_gy.at[d, m], r_gy.at[d, m], ydev(d))
+        send(gg.at[0, 1, 0], gg.at[0, 1, e], s_gf.at[e], r_gf.at[e], zdev(-4 * FAR[e]))
+        for e in range(7, 0, -1)
+    ][::-1]
+    c_gn = []
+    c_gy = []
+
+    def over_y(m, g):
+        e, n = GROUPS[g]
+        return [
+            send(
+                gg.at[0, m, e : e + n], gg.at[d, m, e : e + n], s_gy.at[d, m, g],
+                r_gy.at[d, m, g], ydev(d),
+            )
             for d in range(1, NY)
         ]
+
+    for g in range(5):
+        if g < 4:
+            e, n = GROUPS[g]
+            for c in c_gf[max(e, 1) - 1 : e + n - 1]:
+                c.wait_recv()
+            c_gn.append(
+                [
+                    send(
+                        gg.at[0, 1, e : e + n], gg.at[0, m, e : e + n], s_gn.at[m, g],
+                        r_gn.at[m, g], zdev(-o),
+                    )
+                    for m, o in near
+                ]
+            )
+            c_gy += over_y(1, g)
+        if g > 0:
+            for c, (m, o) in zip(c_gn[g - 1], near):
+                c.wait_recv()
+                c_gy += over_y(m, g - 1)
+    c_gn = [c for some in c_gn for c in some]
 
     by_z = jnp.zeros((1, 128), jnp.float32)
     for k in range(8):
@@ -289,11 +340,11 @@
             val = jnp.sum(
                 jnp.where((lane >= TR) & (lane < TR + 3), row, 0.0), axis=1, keepdims=True
             )
-            by_z = jnp.where(lane == (z + m - 1 + 4 * k + NZ) % NZ, val, by_z)
+            by_z = jnp.where(lane == (z + m - 1 + 4 * FAR[k] + NZ) % NZ, val, by_z)
     loss_ref[...] = jnp.broadcast_to(jnp.sum(by_z, axis=1, keepdims=True), (8, 128))
 
 
-    wl = jnp.concatenate([w_ref[k, m] for k in range(8) for m in range(4)], axis=1)
+    wl = jnp.concatenate([w_ref[FAR[k], m] for k in range(8) for m in range(4)], axis=1)
 
     def grad_block(d):
         gl = jnp.concatenate([gg[d, m, k] for k in range(8) for m in range(4)], axis=1)
@@ -349,11 +400,12 @@
         return carry
 
     lax.fori_loop(0, 2, backward, 0)
+    yb[...] = yy[...].astype(jnp.bfloat16)
     c_gr = [
-        send(yy.at[:, (s + d) % NS], gr.at[d], s_gr.at[d], r_gr.at[d], sdev(d))
+        send(yb.at[:, (s + d) % NS], gr.at[d], s_gr.at[d], r_gr.at[d], sdev(d))
         for d in range(1, NS)
     ]
-    gr[0] = yy[:, s]
+    gr[0] = yb[:, s]
     for c in c_gr:
         c.wait_recv()
     grad_kv = collect(gr) + skip * (oo[...] * query)
@@ -398,14 +450,18 @@
             pltpu.VMEM((8, 2, 16, 128), b16),
             pltpu.VMEM((2, 160, 128), f32),
             pltpu.VMEM((2, 128, 128), f32),
+            pltpu.VMEM((2, 1032, 128), f32),
+            pltpu.VMEM((2, 1024, 256), b16),
+            pltpu.VMEM((8, 256, 256), b16),
             pltpu.VMEM((128, 2048), b16),
             pltpu.VMEM((2, 128, 128, 128), b16),
             pltpu.VMEM((2, 8, 16, 128), f32),
-            pltpu.VMEM((8, 2, 16, 128), f32),
+            pltpu.VMEM((2, 8, 16, 128), b16),
+            pltpu.VMEM((8, 2, 16, 128), b16),
             pltpu.VMEM((256, 128), f32),
             pltpu.VMEM((8, 2, 16, 128), b16),
             pltpu.VMEM((8, 2, 16, 128), b16),
-            pltpu.VMEM((8, 2, 16, 128), f32),
+            pltpu.VMEM((8, 2, 16, 128), b16),
             pltpu.VMEM((4, 16, 128), b16),
             pltpu.VMEM((4, 8, 16, 128), b16),
             pltpu.VMEM((4, 8, 4, 16, 128), b16),
@@ -417,10 +473,10 @@
             sem((2,)),
             sem((8,)), sem((8,)), sem((8,)), sem((8,)), sem((8,)), sem((8,)),
             sem((8,)), sem((8,)), sem((8,)), sem((8,)),
-            sem((4,)), sem((4,)), sem((8,)), sem((8,)), sem((4,)), sem((4,)),
-            sem((4,)), sem((4,)), sem((8,)), sem((8,)), sem((4,)), sem((4,)),
+            sem((4,)), sem((4,)), sem((8,)), sem((8,)), sem((4, 4)), sem((4, 4)),
+            sem((4,)), sem((4,)), sem((8,)), sem((8,)), sem((4, 4)), sem((4, 4)),
             sem((4,)), sem((4,)), sem((8,)), sem((8,)), sem((8,)), sem((8,)),
-            sem((4,)), sem((4,)), sem((4, 4)), sem((4, 4)),
+            sem((4, 4)), sem((4, 4)), sem((4, 4, 4)), sem((4, 4, 4)),
         ],
         compiler_params=pltpu.CompilerParams(collective_id=0, has_side_effects=True),
     )(x, h, skip, w, cnt, bias)

time: 134 us -> 121 us (0.903)
  Pallas kernels: 121 us -> 108 us
    pallas_call x1, Pallas kernels: 121 us -> 108 us  [per_device(): pl.pallas_call(step_kernel, out_shape=(jax.ShapeDtypeStruct((3, 256, 128)...]
where the time goes in v3:
time: 121 us; the launch traced here: 120 us
  Pallas kernels  108 us (89%)
  local copies, waits for them, and re-layouts  9.07 us (7%)
  between operations  2.52 us (2%)
    pallas_call x1, Pallas kernels, per_device(): pl.pallas_call(step_kernel, out_shape=(jax.ShapeDtypeStruct((3, 256, 128)...  108 us

profile of v3, /device:TPU:1, one launch (start us, length us, event | category | flops | bytes accessed | tf_op | source)
XLA Modules:
  0.0 120.4 jit_solution(15053452909766290965)
XLA Ops:
  0.6 0.0 copy-start.1
  0.7 0.8 dynamic_slice.11
  1.5 0.6 broadcast_in_dim.5.bias_ref
  2.1 0.8 dynamic_slice.10
  2.9 0.6 pad.13.cnt_ref
  3.4 0.7 broadcast_in_dim.4
  4.2 0.0 copy-done.1
  4.2 0.0 copy-start.2
  4.2 0.6 copy.11
  4.8 0.7 reshape.32.skip_ref
  5.6 0.0 copy-done.2
  5.6 0.3 reshape.29
  5.9 0.1 copy.9
  6.0 0.0 copy-start
  6.0 0.9 fusion
  6.9 0.0 copy-done
  6.9 0.8 reshape.26.x_ref
  7.7 107.9 %shard_map.77 = (f32[3,256,128]{2,1,0:T(8,128)}, f32[8,128]{1,0:T(8,128)}) custom-call(bf16[3,256,128]{2,1,0:T(8,128)(2,1)} %reshape.26.x_ref, bf16[8,2,16,128]{3,2,1,0:T(8,128)(2,1)} %bitcast.9, f32[256,1]{1,0:T(8,128)} %reshape.32.skip_ref, bf16[8,4,16,128]{3,2,1,0:T(8,128)(2,1)} %bitcast.8, s32[16,128]{1,0:T(8,128)} %pad.13.cnt_ref, ...), custom_call_target="tpu_custom_call" | custom-call | tf_op jit(solution)/shard_map/pallas_call | solution.py:439
  115.6 1.2 slice.3
  117.4 1.8 %reshape.31 = f32[3,16,2048]{2,1,0:T(8,128)} reshape(f32[3,256,128]{2,1,0:T(8,128)} %get-tuple-element.5) | data formatting | bytes 786432 | tf_op jit(solution)/shard_map/reshape | solution.py:484
  (3 shorter events, 0.0 us)
Async XLA Ops:
  0.6 3.5 %copy-start.1 = (f32[16,2048]{1,0:T(8,128)S(1)}, f32[16,2048]{1,0:T(8,128)}, u32[]{:S(2)}) copy-start(f32[16,2048]{1,0:T(8,128)} %param.7) | copy-start | bytes 393220
  4.2 1.4 %copy-start.2 = (bf16[16,3840]{1,0:T(8,128)(2,1)S(1)}, bf16[16,3840]{1,0:T(8,128)(2,1)}, u32[]{:S(2)}) copy-start(bf16[16,3840]{1,0:T(8,128)(2,1)} %param.9) | copy-start | bytes 368644
  6.0 0.9 copy-start

commit v4 on v3

--- a/solution.py
+++ b/solution.py
@@ -19,13 +19,13 @@
 
 
 def step_kernel(
-    x_ref, h_ref, skip_ref, w_ref, cnt_ref, bias_ref,
+    proj_ref, taps_ref, skip_ref, head_ref, count_ref, bias_ref,
     out_ref, loss_ref,
-    kv, hx, rx, xp, hf, vf, vb, pick, sh, tt, yy, yb, cv, oo, gx, gg_out, gr, pp,
-    wa, wg, py, pg, ty, ts, gg,
+    x_ref, ht, h_ref, w_ref, cnt_ref, mx, kv, hx, rx, xp, hf, vf, vb, pick, sh, tt, yy, yb, cv, oo, gx, gg_out, gr, pp,
+    wa, wg, py, pg, ty, gg,
     s_loc, s_kv, r_kv, s_hx, r_hx, s_cv, r_cv, s_gx, r_gx, s_gr, r_gr,
     s_wa, r_wa, s_wb, r_wb, s_wy, r_wy, s_py, r_py, s_pf, r_pf, s_pn, r_pn,
-    s_ty, r_ty, s_ts, r_ts, s_gf, r_gf, s_gn, r_gn, s_gy, r_gy,
+    s_ty, r_ty, s_gf, r_gf, s_gn, r_gn, s_gy, r_gy,
 ):
     s = lax.axis_index("seq")
     ch = lax.axis_index("chan")
@@ -40,6 +40,9 @@
 
     def sdev(d):
         return ((s + d) % NS, ch)
+
+    def both_dev(a, b):
+        return ((s + b) % NS, ((y + a) % NY) * NZ + z)
 
     def send(src, dst, ss, rs, dev):
         c = pltpu.make_async_remote_copy(
@@ -51,13 +54,35 @@
     near = ((0, -1), (2, 1), (3, 2))
 
     barrier = pltpu.get_barrier_semaphore()
-    peers = [sdev(d) for d in range(1, NS)] + [ydev(d) for d in range(1, NY)]
+    group = [(a, b) for a in range(NY) for b in range(NS) if a or b]
+    peers = [both_dev(a, b) for a, b in group]
     peers += [zdev(4 * k) for k in range(1, 8)] + [zdev(d) for d in (-2, -1, 1, 2)]
     for dev in peers:
         pl.semaphore_signal(barrier, inc=1, device_id=dev, device_id_type=MESH)
 
 
-    key_value = x_ref[1].astype(jnp.float32) * x_ref[2].astype(jnp.float32)
+    base = 120 * z // 128 - z // 31
+    shift = (256 - (120 * z - 128 * base)) % 256
+    base = pl.multiple_of(128 * base, 128)
+    c_cnt = pltpu.make_async_copy(
+        count_ref.at[pl.ds(pl.multiple_of(16 * y, 16), 16), pl.ds(base, 256)], cnt_ref, s_loc.at[2]
+    )
+    c_cnt.start()
+    for a in range(16):
+        for p in range(3):
+            x_ref[p, pl.ds(a, 16, stride=16), :] = proj_ref[
+                p, :, 128 * a : 128 * a + 128
+            ].astype(jnp.float32)
+        ht[pl.ds(a, 16, stride=16), :] = taps_ref[:, 128 * a : 128 * a + 128]
+    h_ref[...] = ht[...].astype(jnp.bfloat16).reshape(NS, 2, 16, 128)
+    tile_lane = lax.broadcasted_iota(jnp.int32, (16, 128), 1)
+    for t in range(NZ):
+        first = min(TR * t // 128, 28) * 128
+        tile = head_ref[:, first : first + 256].astype(jnp.float32)
+        tile = pltpu.roll(tile, (256 - (TR * t - first)) % 256, 1)[:, :128]
+        at = (t + NZ + 1 - z) % NZ
+        w_ref[at // 4, at % 4] = jnp.where(tile_lane < TR, tile, 0.0).astype(jnp.bfloat16)
+    key_value = x_ref[1] * x_ref[2]
     kv[...] = key_value.astype(jnp.bfloat16).reshape(NS, 2, 16, 128)
     for c in range(2):
         xp[c, 0:16, :] = jnp.zeros((16, 128), jnp.float32)
@@ -179,11 +204,13 @@
             [blocks[(s + NS - a) % NS].astype(jnp.float32).reshape(32, 128) for a in range(NS)], axis=0
         )
 
-    skip = skip_ref[...]
-    query = x_ref[0].astype(jnp.float32)
+    skip = jnp.concatenate(
+        [jnp.full((16, 128), skip_ref[c], jnp.float32) for c in range(16)], axis=0
+    )
+    query = x_ref[0]
     mixed = collect(cv) + skip * key_value
     oo[...] = query * mixed
-    out_ref[0] = mixed
+    mx[...] = mixed
 
     small_row = lax.broadcasted_iota(jnp.int32, (16, 128), 0)
     small_col = lax.broadcasted_iota(jnp.int32, (16, 128), 1)
@@ -246,7 +273,9 @@
     for c in c_wy:
         c.wait_recv()
 
-    logits = jnp.broadcast_to(bias_ref[0:1, :], (16, 128))
+    bias = jnp.broadcast_to(bias_ref[0:1, pl.ds(base, 256)], (16, 256))
+    bias = pltpu.roll(bias, shift, 1)[:, :128]
+    logits = jnp.where(tile_lane < TR, bias, 0.0)
     for k in range(8):
         for m in range(4):
             rows = jnp.concatenate([wg[d, k, m] for d in range(NY)], axis=0)
@@ -255,29 +284,28 @@
                 preferred_element_type=jnp.float32,
             )
     rates = jnp.maximum(logits, 0.0) + jnp.log1p(jnp.exp(-jnp.abs(logits))) + rate_floor
-    observed = cnt_ref[...].astype(jnp.float32)
+    c_cnt.wait()
+    observed = pltpu.roll(cnt_ref[...].astype(jnp.float32), shift, 1)[:, :128]
+    observed = jnp.where(tile_lane < TR, observed, 0.0)
     part = [
         jnp.sum(rates, axis=0, keepdims=True),
         jnp.sum(observed, axis=0, keepdims=True),
         jnp.sum(observed * jnp.log(rates), axis=0, keepdims=True),
         jnp.zeros((5, 128), jnp.float32),
     ]
-    ty[0] = jnp.concatenate(part, axis=0)
-    c_ty = [send(ty.at[0], ty.at[d], s_ty.at[d], r_ty.at[d], ydev(d)) for d in range(1, NY)]
+    ty[0, 0] = jnp.concatenate(part, axis=0)
+    c_ty = [
+        send(ty.at[0, 0], ty.at[a, b], s_ty.at[a, b], r_ty.at[a, b], both_dev(a, b))
+        for a, b in group
+    ]
     sig = 1.0 / (1.0 + jnp.exp(-logits))
     obs_rate = observed / rates
     for c in c_ty:
         c.wait_recv()
-    tot = ty[y]
-    for a in range(1, NY):
-        tot = tot + ty[(y + NY - a) % NY]
-    ts[0] = tot
-    c_ts = [send(ts.at[0], ts.at[d], s_ts.at[d], r_ts.at[d], sdev(d)) for d in range(1, NS)]
-    for c in c_ts:
-        c.wait_recv()
-    tot = ts[s]
-    for a in range(1, NS):
-        tot = tot + ts[(s + NS - a) % NS]
+    tot = jnp.zeros((8, 128), jnp.float32)
+    for a in range(NY):
+        for b in range(NS):
+            tot = tot + ty[(y + NY - a) % NY, (s + NS - b) % NS]
     pred = tot[0:1, :]
     obs = tot[1:2, :]
     log_pred = jnp.log(pred)
@@ -341,7 +369,7 @@
                 jnp.where((lane >= TR) & (lane < TR + 3), row, 0.0), axis=1, keepdims=True
             )
             by_z = jnp.where(lane == (z + m - 1 + 4 * FAR[k] + NZ) % NZ, val, by_z)
-    loss_ref[...] = jnp.broadcast_to(jnp.sum(by_z, axis=1, keepdims=True), (8, 128))
+    loss_ref[0, 0] = jnp.sum(by_z) * (1.0 / (512 * 3840))
 
 
     wl = jnp.concatenate([w_ref[FAR[k], m] for k in range(8) for m in range(4)], axis=1)
@@ -368,7 +396,13 @@
         for d in range(1, NS)
     ]
     gx[0] = gg_out[s]
-    out_ref[0] = oo[...] * out_ref[0]
+
+    def give(p):
+        for a in range(16):
+            out_ref[p, :, 128 * a : 128 * a + 128] = mx[pl.ds(a, 16, stride=16), :]
+
+    mx[...] = oo[...] * mx[...]
+    give(0)
     for c in c_cv:
         c.wait_send()
     for c in c_gx:
@@ -409,42 +443,42 @@
     for c in c_gr:
         c.wait_recv()
     grad_kv = collect(gr) + skip * (oo[...] * query)
-    out_ref[1] = grad_kv * x_ref[2].astype(jnp.float32)
-    out_ref[2] = grad_kv * x_ref[1].astype(jnp.float32)
-
-    for c in c_hx + c_kv + c_wa + c_py + c_wb + c_pf + c_pn + c_wy + c_ty + c_ts:
+    mx[...] = grad_kv * x_ref[2]
+    give(1)
+    mx[...] = grad_kv * x_ref[1]
+    give(2)
+
+    for c in c_hx + c_kv + c_wa + c_py + c_wb + c_pf + c_pn + c_wy + c_ty:
         c.wait_send()
     for c in c_gf + c_gn + c_gy + c_gx + c_gr:
         c.wait_send()
 
 
 def per_device(projections, filter_taps, skip_gain, head_weight, head_bias, counts):
-    ch = lax.axis_index("chan")
-    y = ch // NZ
-    z = ch % NZ
-    x = projections.reshape(3, 256, 128)
-    h = filter_taps.astype(jnp.bfloat16).reshape(NS, 2, 16, 128)
-    skip = jnp.broadcast_to(skip_gain[:, None], (16, 16)).reshape(256, 1)
-    w = jnp.pad(head_weight.reshape(16, NZ, TR), ((0, 0), (0, 0), (0, 128 - TR)))
-    w = jnp.transpose(w, (1, 0, 2))
-    w = lax.dynamic_slice_in_dim(jnp.concatenate([w, w], axis=0), (z + NZ - 1) % NZ, NZ, 0)
-    w = w.reshape(8, 4, 16, 128)
-    cnt = lax.dynamic_slice(counts, (y * 16, z * TR), (16, TR))
-    cnt = jnp.pad(cnt, ((0, 0), (0, 128 - TR)))
-    bias = jnp.pad(lax.dynamic_slice_in_dim(head_bias, z * TR, TR, 0), (0, 128 - TR))
-    bias = jnp.broadcast_to(bias[None, :], (8, 128))
     sem = pltpu.SemaphoreType.DMA
     b16 = jnp.bfloat16
     f32 = jnp.float32
     out, loss = pl.pallas_call(
         step_kernel,
         out_shape=(
-            jax.ShapeDtypeStruct((3, 256, 128), f32),
-            jax.ShapeDtypeStruct((8, 128), f32),
+            jax.ShapeDtypeStruct((3, 16, 2048), f32),
+            jax.ShapeDtypeStruct((1, 1), f32),
         ),
-        in_specs=[pl.BlockSpec(memory_space=pltpu.VMEM)] * 6,
-        out_specs=(pl.BlockSpec(memory_space=pltpu.VMEM),) * 2,
+        in_specs=[
+            pl.BlockSpec(memory_space=space)
+            for space in (pltpu.VMEM, pltpu.VMEM, pltpu.SMEM, pltpu.VMEM, pl.ANY, pltpu.VMEM)
+        ],
+        out_specs=(
+            pl.BlockSpec(memory_space=pltpu.VMEM),
+            pl.BlockSpec(memory_space=pltpu.SMEM),
+        ),
         scratch_shapes=[
+            pltpu.VMEM((3, 256, 128), f32),
+            pltpu.VMEM((256, 128), f32),
+            pltpu.VMEM((8, 2, 16, 128), b16),
+            pltpu.VMEM((8, 4, 16, 128), b16),
+            pltpu.VMEM((16, 256), jnp.int32),
+            pltpu.VMEM((256, 128), f32),
             pltpu.VMEM((8, 2, 16, 128), b16),
             pltpu.VMEM((7, 2, 16, 128), b16),
             pltpu.VMEM((8, 2, 16, 128), b16),
@@ -467,21 +501,19 @@
             pltpu.VMEM((4, 8, 4, 16, 128), b16),
             pltpu.VMEM((3, 16, 128), b16),
             pltpu.VMEM((4, 8, 16, 128), b16),
-            pltpu.VMEM((4, 8, 128), f32),
-            pltpu.VMEM((8, 8, 128), f32),
+            pltpu.VMEM((4, 8, 8, 128), f32),
             pltpu.VMEM((4, 4, 8, 16, 128), b16),
-            sem((2,)),
+            sem((3,)),
             sem((8,)), sem((8,)), sem((8,)), sem((8,)), sem((8,)), sem((8,)),
             sem((8,)), sem((8,)), sem((8,)), sem((8,)),
             sem((4,)), sem((4,)), sem((8,)), sem((8,)), sem((4, 4)), sem((4, 4)),
             sem((4,)), sem((4,)), sem((8,)), sem((8,)), sem((4, 4)), sem((4, 4)),
-            sem((4,)), sem((4,)), sem((8,)), sem((8,)), sem((8,)), sem((8,)),
+            sem((4, 8)), sem((4, 8)), sem((8,)), sem((8,)),
             sem((4, 4)), sem((4, 4)), sem((4, 4, 4)), sem((4, 4, 4)),
         ],
         compiler_params=pltpu.CompilerParams(collective_id=0, has_side_effects=True),
-    )(x, h, skip, w, cnt, bias)
-    mean_loss = loss[0, 0] / (512 * 3840)
-    return mean_loss, out.reshape(3, 16, 2048)
+    )(projections, filter_taps, skip_gain, head_weight, counts, head_bias.reshape(1, -1))
+    return loss.reshape(()), out
 
 
 def solution(mesh):

time: 121 us -> 113 us (0.934)
  local copies, waits for them, and re-layouts: 9.07 us -> 3.1 us
    reshape x5 -> x1, local copies, waits for them, and re-layouts: 3.69 us -> 1.33 us  [per_device(): head_bias.reshape(1, -1)]
    dynamic_slice x2 -> x0, local copies, waits for them, and re-layouts: 1.57 us -> none  [the longest x1 0.79 us: per_device(): cnt = lax.dynamic_slice(counts, (y * 16, z * TR), (16, TR))]
    broadcast_in_dim x2 -> x0, local copies, waits for them, and re-layouts: 1.32 us -> none  [the longest x1 0.72 us: per_device(): skip = jnp.broadcast_to(skip_gain[:, None], (16, 16)).reshape(256, 1)]
where the time goes in v4:
time: 113 us; the launch traced here: 112 us
  Pallas kernels  107 us (95%)
  local copies, waits for them, and re-layouts  3.1 us (3%)
  between operations  2.39 us (2%)
    pallas_call x1, Pallas kernels, per_device(): pl.pallas_call(step_kernel, out_shape=(jax.ShapeDtypeStruct((3, 16, 2048)...  107 us

profile of v4, /device:TPU:1, one launch (start us, length us, event | category | flops | bytes accessed | tf_op | source)
XLA Modules:
  0.0 112.5 jit_solution(11654150763366737545)
XLA Ops:
  0.6 1.3 %reshape.10.bias_ref = f32[1,3840]{1,0:T(1,128)} reshape(f32[3840]{0:T(1024)} %param.10) | data formatting | bytes 30720 | tf_op jit(solution)/shard_map/reshape | solution.py:515
  2.0 107.0 %shard_map.77 = (f32[3,16,2048]{2,1,0:T(8,128)}, f32[1,1]{1,0:T(1,128)}) custom-call(bf16[3,16,2048]{2,1,0:T(8,128)(2,1)} %proj_ref.1, f32[16,2048]{1,0:T(8,128)} %taps_ref.1, f32[16]{0:T(128)} %skip_ref.1, bf16[16,3840]{1,0:T(8,128)(2,1)} %head_ref.1, s32[64,3840]{1,0:T(8,128)} %count_ref.1, f32[1,3840]{1,0:T(1,128)} %reshape.10.bias_ref), custom_call_target="tpu_custom_call" | custom-call | tf_op jit(solution)/shard_map/pallas_call | solution.py:461
  109.6 1.8 %copy.11 = f32[3,16,2048]{2,1,0:T(8,128)} copy(f32[3,16,2048]{2,1,0:T(8,128)} %get-tuple-element.9) | data formatting | bytes 786432

commit v5 on v4

--- a/solution.py
+++ b/solution.py
@@ -23,7 +23,7 @@
     out_ref, loss_ref,
     x_ref, ht, h_ref, w_ref, cnt_ref, mx, kv, hx, rx, xp, hf, vf, vb, pick, sh, tt, yy, yb, cv, oo, gx, gg_out, gr, pp,
     wa, wg, py, pg, ty, gg,
-    s_loc, s_kv, r_kv, s_hx, r_hx, s_cv, r_cv, s_gx, r_gx, s_gr, r_gr,
+    entered, s_loc, s_kv, r_kv, s_hx, r_hx, s_cv, r_cv, s_gx, r_gx, s_gr, r_gr,
     s_wa, r_wa, s_wb, r_wb, s_wy, r_wy, s_py, r_py, s_pf, r_pf, s_pn, r_pn,
     s_ty, r_ty, s_gf, r_gf, s_gn, r_gn, s_gy, r_gy,
 ):
@@ -55,8 +55,8 @@
 
     barrier = pltpu.get_barrier_semaphore()
     group = [(a, b) for a in range(NY) for b in range(NS) if a or b]
-    peers = [both_dev(a, b) for a, b in group]
-    peers += [zdev(4 * k) for k in range(1, 8)] + [zdev(d) for d in (-2, -1, 1, 2)]
+    peers = [sdev(d) for d in range(1, NS)] + [ydev(d) for d in range(1, NY)]
+    peers += [zdev(d) for d in (-2, -1, 1, 2)]
     for dev in peers:
         pl.semaphore_signal(barrier, inc=1, device_id=dev, device_id_type=MESH)
 
@@ -96,6 +96,18 @@
         ).astype(jnp.bfloat16)
     pl.semaphore_wait(barrier, len(peers))
 
+    def tell(step):
+        for side in range(2):
+            pl.semaphore_signal(
+                entered.at[step, side], inc=1, device_id=zdev((2 - 4 * side) * 2**step),
+                device_id_type=MESH,
+            )
+
+    def hear(step):
+        for side in range(2):
+            pl.semaphore_wait(entered.at[step, side], 1)
+
+    tell(0)
     c_hx = [
         send(h_ref.at[(s + d) % NS], hx.at[d - 1], s_hx.at[d], r_hx.at[d], sdev(d))
         for d in range(1, NS)
@@ -109,16 +121,6 @@
     for c in c_hx:
         c.wait_recv()
 
-    own_wa.wait()
-    for c in c_wa:
-        c.wait_recv()
-    c_wb = [
-        send(wa.at[:, FAR[e]], wg.at[0, e], s_wb.at[e], r_wb.at[e], zdev(4 * FAR[e]))
-        for e in range(7, 0, -1)
-    ][::-1]
-    own_wb = pltpu.make_async_copy(wa.at[:, 0], wg.at[0, 0], s_loc.at[1])
-    own_wb.start()
-
     def put_taps(d, block):
         a = pl.multiple_of((s + NS - d) % NS * 16, 16)
         for c in range(2):
@@ -127,6 +129,8 @@
     put_taps(0, h_ref[s])
     for d in range(1, NS):
         put_taps(d, hx[d - 1])
+    hear(0)
+    tell(1)
 
     lane8 = lax.broadcasted_iota(jnp.int32, (8, 128), 1)
     sub8 = lax.broadcasted_iota(jnp.int32, (8, 128), 0)
@@ -146,6 +150,8 @@
 
     windows(0)
     windows(1)
+    hear(1)
+    tell(2)
 
     def fill(q, carry):
         for c in range(2):
@@ -196,6 +202,16 @@
         for d in range(1, NS)
     ]
     cv[0] = yb[:, s]
+    hear(2)
+    own_wa.wait()
+    for c in c_wa:
+        c.wait_recv()
+    c_wb = [
+        send(wa.at[:, FAR[e]], wg.at[0, e], s_wb.at[e], r_wb.at[e], zdev(4 * FAR[e]))
+        for e in range(7, 0, -1)
+    ][::-1]
+    own_wb = pltpu.make_async_copy(wa.at[:, 0], wg.at[0, 0], s_loc.at[1])
+    own_wb.start()
     for c in c_cv:
         c.wait_recv()
 
@@ -273,7 +289,9 @@
     for c in c_wy:
         c.wait_recv()
 
-    bias = jnp.broadcast_to(bias_ref[0:1, pl.ds(base, 256)], (16, 256))
+    line = base // 128
+    bias = jnp.concatenate([bias_ref[pl.ds(line + a, 1), :] for a in range(2)], axis=1)
+    bias = jnp.broadcast_to(bias, (16, 256))
     bias = pltpu.roll(bias, shift, 1)[:, :128]
     logits = jnp.where(tile_lane < TR, bias, 0.0)
     for k in range(8):
@@ -503,6 +521,7 @@
             pltpu.VMEM((4, 8, 16, 128), b16),
             pltpu.VMEM((4, 8, 8, 128), f32),
             pltpu.VMEM((4, 4, 8, 16, 128), b16),
+            pltpu.SemaphoreType.REGULAR((3, 2)),
             sem((3,)),
             sem((8,)), sem((8,)), sem((8,)), sem((8,)), sem((8,)), sem((8,)),
             sem((8,)), sem((8,)), sem((8,)), sem((8,)),
@@ -512,7 +531,7 @@
             sem((4, 4)), sem((4, 4)), sem((4, 4, 4)), sem((4, 4, 4)),
         ],
         compiler_params=pltpu.CompilerParams(collective_id=0, has_side_effects=True),
-    )(projections, filter_taps, skip_gain, head_weight, counts, head_bias.reshape(1, -1))
+    )(projections, filter_taps, skip_gain, head_weight, counts, head_bias.reshape(-1, 128))
     return loss.reshape(()), out
 
 

time: 113 us -> 108 us (0.956)
  Pallas kernels: 107 us -> 104 us
  local copies, waits for them, and re-layouts: 3.1 us -> 1.77 us
    pallas_call x1, Pallas kernels: 107 us -> 104 us  [per_device(): pl.pallas_call(step_kernel, out_shape=(jax.ShapeDtypeStruct((3, 16, 2048)...]
    reshape x1 -> x0, local copies, waits for them, and re-layouts: 1.33 us -> none  [per_device(): head_bias.reshape(1, -1)]
where the time goes in v5:
time: 108 us
  Pallas kernels  104 us (96%)
  between operations  2.39 us (2%)
  local copies, waits for them, and re-layouts  1.77 us (2%)
    pallas_call x1, Pallas kernels, per_device(): pl.pallas_call(step_kernel, out_shape=(jax.ShapeDtypeStruct((3, 16, 2048)...  104 us

profile of v5, /device:TPU:1, one launch (start us, length us, event | category | flops | bytes accessed | tf_op | source)
XLA Modules:
  0.0 107.7 jit_solution(1937032627942336345)
XLA Ops:
  0.6 103.5 %shard_map.77 = (f32[3,16,2048]{2,1,0:T(8,128)}, f32[1,1]{1,0:T(1,128)}) custom-call(bf16[3,16,2048]{2,1,0:T(8,128)(2,1)} %proj_ref.1, f32[16,2048]{1,0:T(8,128)} %taps_ref.1, f32[16]{0:T(128)} %skip_ref.1, bf16[16,3840]{1,0:T(8,128)(2,1)} %head_ref.1, s32[64,3840]{1,0:T(8,128)} %count_ref.1, f32[30,128]{1,0:T(8,128)} %bitcast.2), custom_call_target="tpu_custom_call" | custom-call | tf_op jit(solution)/shard_map/pallas_call | solution.py:479
  104.8 1.8 %copy.11 = f32[3,16,2048]{2,1,0:T(8,128)} copy(f32[3,16,2048]{2,1,0:T(8,128)} %get-tuple-element.9) | data formatting | bytes 786432

commit v6 on v5

--- a/solution.py
+++ b/solution.py
@@ -162,7 +162,7 @@
             tt[c, :, pl.ds(pl.multiple_of(16 * q, 16), 16), :] = both.astype(jnp.bfloat16)
         return carry
 
-    lax.fori_loop(0, 8, fill, 0)
+    lax.fori_loop(0, 8, fill, 0, unroll=4)
 
     def place(blocks):
         for a in range(NS):
@@ -178,14 +178,14 @@
 
     def forward(c, carry):
         for d in range(16):
-            sh[:, 128 * d : 128 * d + 128] = xp[c, 16 - d : 144 - d, :].astype(jnp.bfloat16)
+            sh[c, :, 128 * d : 128 * d + 128] = xp[c, 16 - d : 144 - d, :].astype(jnp.bfloat16)
         for p in range(4):
             taps = jnp.concatenate(
                 [tt[c, 32 * p + 16 * h : 32 * p + 16 * h + 16].reshape(2048, 128) for h in range(2)],
                 axis=1,
             )
             rows = 128 - 32 * p
-            part = jnp.dot(sh[0:rows, :], taps, preferred_element_type=jnp.float32)
+            part = jnp.dot(sh[c, 0:rows, :], taps, preferred_element_type=jnp.float32)
             first = part[:, :128].reshape(8 - 2 * p, 16, 128)
             second = part[: rows - 16, 128:].reshape(7 - 2 * p, 16, 128)
             if p == 0:
@@ -195,7 +195,8 @@
             yy[c, 2 * p + 1 : 8] = yy[c, 2 * p + 1 : 8] + second
         return carry
 
-    lax.fori_loop(0, 2, forward, 0)
+    for c in range(2):
+        forward(c, 0)
     yb[...] = yy[...].astype(jnp.bfloat16)
     c_cv = [
         send(yb.at[:, (s + d) % NS], cv.at[d], s_cv.at[d], r_cv.at[d], sdev(d))
@@ -429,7 +430,7 @@
 
     def backward(c, carry):
         for d in range(16):
-            sh[:, 128 * d : 128 * d + 128] = xp[c, 16 + d : 144 + d, :].astype(jnp.bfloat16)
+            sh[c, :, 128 * d : 128 * d + 128] = xp[c, 16 + d : 144 + d, :].astype(jnp.bfloat16)
         for p in range(4):
             taps = jnp.concatenate(
                 [
@@ -440,7 +441,7 @@
             )
             rows = 128 - 32 * p
             part = lax.dot_general(
-                sh[32 * p : 128, :], taps, nt, preferred_element_type=jnp.float32
+                sh[c, 32 * p : 128, :], taps, nt, preferred_element_type=jnp.float32
             )
             first = part[:, :128].reshape(8 - 2 * p, 16, 128)
             second = part[16:, 128:].reshape(7 - 2 * p, 16, 128)
@@ -451,7 +452,8 @@
             yy[c, 0 : 7 - 2 * p] = yy[c, 0 : 7 - 2 * p] + second
         return carry
 
-    lax.fori_loop(0, 2, backward, 0)
+    for c in range(2):
+        backward(c, 0)
     yb[...] = yy[...].astype(jnp.bfloat16)
     c_gr = [
         send(yb.at[:, (s + d) % NS], gr.at[d], s_gr.at[d], r_gr.at[d], sdev(d))
@@ -505,7 +507,7 @@
             pltpu.VMEM((2, 1032, 128), f32),
             pltpu.VMEM((2, 1024, 256), b16),
             pltpu.VMEM((8, 256, 256), b16),
-            pltpu.VMEM((128, 2048), b16),
+            pltpu.VMEM((2, 128, 2048), b16),
             pltpu.VMEM((2, 128, 128, 128), b16),
             pltpu.VMEM((2, 8, 16, 128), f32),
             pltpu.VMEM((2, 8, 16, 128), b16),

time: 108 us -> 107 us (level)
  no operation moved by 1% of the time
where the time goes in v6:
time: 107 us
  Pallas kernels  103 us (96%)
  between operations  2.39 us (2%)
  local copies, waits for them, and re-layouts  1.77 us (2%)
    pallas_call x1, Pallas kernels, per_device(): pl.pallas_call(step_kernel, out_shape=(jax.ShapeDtypeStruct((3, 16, 2048)...  103 us

profile of v6, /device:TPU:1, one launch (start us, length us, event | category | flops | bytes accessed | tf_op | source)
XLA Modules:
  0.0 107.0 jit_solution(15640275297122909128)
XLA Ops:
  0.6 102.8 %shard_map.77 = (f32[3,16,2048]{2,1,0:T(8,128)}, f32[1,1]{1,0:T(1,128)}) custom-call(bf16[3,16,2048]{2,1,0:T(8,128)(2,1)} %proj_ref.1, f32[16,2048]{1,0:T(8,128)} %taps_ref.1, f32[16]{0:T(128)} %skip_ref.1, bf16[16,3840]{1,0:T(8,128)(2,1)} %head_ref.1, s32[64,3840]{1,0:T(8,128)} %count_ref.1, f32[30,128]{1,0:T(8,128)} %bitcast.2), custom_call_target="tpu_custom_call" | custom-call | tf_op jit(solution)/shard_map/pallas_call | solution.py:481
  104.1 1.8 %copy.11 = f32[3,16,2048]{2,1,0:T(8,128)} copy(f32[3,16,2048]{2,1,0:T(8,128)} %get-tuple-element.9) | data formatting | bytes 786432
